TPU v7x, 32 devices: a whole 2x2x4 slice. The times are simulated.
32 devices in a mesh: grp: 2 (over x), chan: 16 (over z, y, core).
Axes of the slice: x: 2, y: 2, z: 4, core: 2. Of those that a mesh axis runs over, the one named last changes fastest.
Arguments:
- voltages: bfloat16 [8, 16384, 2048], P('grp', 'chan'), parts along dimension 0, may hold values from -6 to 6
- delay_step: int32 [16384], replicated, may hold values from 0 to 1048575
- trials: int32 [256], replicated, may hold values from 0 to 2047
Outputs:
- spectra: float32 [48, 2, 8, 256], P('chan', None, 'grp'), parts along dimension 2
- power: float32 [8, 256], P('grp', 'chan'), parts along dimension 0
There are 2 independent parts, one for each index of `grp`. A program takes and returns all parts, laid end to end along the dimension named above; an argument that names none is the same for every part. Nothing has to cross between parts.
All inputs are finite; a program needn't handle non-finite values.
Results may differ from a plain program's by a relative error of at most 0.0037.
Values may be sent and summed in bfloat16 or wider, within the bound.
No kernel may reach another device: no remote copies, remote signals or barrier semaphores. Data moves between devices by JAX's collectives and lax.ppermute only.
A program may use at most 64 MiB of HBM per device.

v0:
```python
import math

import jax
import jax.numpy as jnp
from jax import lax
from jax.sharding import PartitionSpec as P

SUBSTEPS = 512
SPIN_DEV = 3


def build_table(samples, bins):
    times = jnp.arange(samples, dtype=jnp.int32)
    frequency = jnp.arange(bins, dtype=jnp.int32)
    phase_index = times[:, None] * frequency[None, :] % samples
    angles = phase_index.astype(jnp.float32) * (2.0 * math.pi / samples)
    return jnp.concatenate([jnp.cos(angles), -jnp.sin(angles)], axis=1).astype(jnp.bfloat16)


def make_phases(spin_bin, delay_step, trials, modulus):
    chan_phase = spin_bin * delay_step % modulus
    phase_index = chan_phase[:, None] * trials[None, :] % modulus
    angles = phase_index.astype(jnp.float32) * (2.0 * math.pi / modulus)
    return jnp.concatenate([jnp.cos(angles), jnp.sin(angles)], axis=1)


def dedisperse(pair_rows, spin_bin, delay_step, trials, modulus, beam_count, chan_scale):
    rows_wide = pair_rows.astype(jnp.float32)
    half_count = trials.shape[0] // 2
    pieces = []
    for half_index in range(2):
        trial_half = trials[half_index * half_count : (half_index + 1) * half_count]
        phases = make_phases(spin_bin, delay_step, trial_half, modulus)
        product = jnp.dot(
            rows_wide, phases, precision=lax.Precision.HIGHEST, preferred_element_type=jnp.float32
        )
        real_rows = product[:beam_count]
        imag_rows = product[beam_count:]
        real_out = real_rows[:, :half_count] - imag_rows[:, half_count:]
        imag_out = real_rows[:, half_count:] + imag_rows[:, :half_count]
        pieces.append(jnp.stack([real_out, imag_out]))
    return jnp.concatenate(pieces, axis=2) * chan_scale


def per_device(voltages, delay_step, trials):
    beam_count, local_chan, samples = voltages.shape
    modulus = samples * SUBSTEPS
    chan_count = lax.axis_size("chan")
    bins_total = SPIN_DEV * chan_count
    all_chan = delay_step.shape[0]
    chan_scale = 1.0 / math.sqrt(all_chan)
    dft_table = build_table(samples, bins_total)
    spectrum = lax.dot_general(
        dft_table, voltages, (((0,), (2,)), ((), ())), preferred_element_type=jnp.float32
    )
    spectrum = (spectrum * (1.0 / math.sqrt(samples))).astype(jnp.bfloat16)
    spectrum = spectrum.reshape(2, bins_total, beam_count, local_chan)
    regrouped = lax.all_to_all(spectrum, "chan", split_axis=1, concat_axis=3, tiled=True)
    first_bin = lax.axis_index("chan") * SPIN_DEV

    def one_bin(offset):
        pair_rows = lax.dynamic_index_in_dim(regrouped, offset, axis=1, keepdims=False).reshape(
            2 * beam_count, all_chan
        )
        return dedisperse(
            pair_rows, first_bin + offset, delay_step, trials, modulus, beam_count, chan_scale
        )

    spectra = lax.map(one_bin, jnp.arange(SPIN_DEV, dtype=jnp.int32))
    power_part = jnp.sum(spectra * spectra, axis=(0, 1)) / bins_total
    power_out = lax.psum_scatter(power_part, "chan", scatter_dimension=1, tiled=True)
    return (spectra, power_out)


def solution(mesh):
    return jax.shard_map(
        per_device,
        mesh=mesh,
        in_specs=(P("grp", "chan", None), P(), P()),
        out_specs=(P("chan", None, "grp", None), P("grp", "chan")),
        check_vma=False,
    )
```

profile of v0, /device:TPU:0, one launch (start us, length us, event | category | flops | bytes accessed | tf_op | source)
XLA Modules:
  0.0 369.8 jit_solution(14272384766015729863)
XLA Ops:
  7.2 1.6 negate_convert_fusion
  8.8 0.0 copy-start
  8.8 0.0 copy-start.1
  8.8 11.1 %multiply_convert_fusion = bf16[96,4,1024]{2,0,1:T(8,128)(2,1)S(1)} fusion(bf16[4,1024,2048]{2,1,0:T(8,128)(2,1)} %param.5, bf16[2048,48]{0,1:T(8,128)(2,1)S(1)} %get-tuple-element.121, bf16[2048,48]{0,1:T(8,128)(2,1)S(1)} %get-tuple-element.122), kind=kOutput, calls=%fused_computation.47 | convolution fusion | flops 1612185600 | bytes 17956864 | tf_op jit(solution)/shard_map/dot_general | solution.py:53
  19.9 1.5 copy.9
  21.4 7.4 %all-to-all-start = ((bf16[2,48,4,1024]{3,2,0,1:T(4,128)(2,1)}), bf16[2,48,4,1024]{3,2,0,1:T(4,128)(2,1)S(1)}, u32[]{:S(2)}, u32[]{:S(2)}) async-start(bf16[2,48,4,1024]{3,2,0,1:T(4,128)(2,1)} %copy.9), calls=%async_computation | async-start | bytes 1572864 | tf_op jit(solution)/shard_map/all_to_all | solution.py:58
  28.8 0.0 reduce-scatter.4.cloned.1.call-start
  28.8 18.6 %all-to-all-done = bf16[2,48,4,1024]{3,2,0,1:T(4,128)(2,1)S(1)} async-done(((bf16[2,48,4,1024]{3,2,0,1:T(4,128)(2,1)}), bf16[2,48,4,1024]{3,2,0,1:T(4,128)(2,1)S(1)}, u32[]{:S(2)}, u32[]{:S(2)}) %all-to-all-start) | async-done | bytes 786464 | tf_op jit(solution)/shard_map/all_to_all | solution.py:58
  47.5 0.4 copy.11
  47.9 0.6 all_to_all.16
  48.5 0.0 copy-done
  48.5 0.0 copy-done.1
  48.5 256.2 %while.12 = (s32[]{:T(128)}, f32[3,2,4,256]{3,2,1,0:T(4,128)S(1)}, s32[3]{0:T(128)S(1)}, bf16[2,3,4,16384]{3,2,1,0:T(4,128)(2,1)S(1)}, s32[]{:T(128)}, /*index=5...) while((s32[]{:T(128)}, f32[3,2,4,256]{3,2,1,0:T(4,128)S(1)}, s32[3]{0:T(128)S(1)}, ...), condition=%wide.region_1.2_spmd, body=%wide.region_0.1_spmd.sunk | while | flops 872620032 | bytes 68955304 | solution.py:69
  48.7 0.6 dynamic_slice.18
  51.2 0.1 constant_dynamic-slice_fusion.2
  51.3 0.1 reshape.66
  52.1 67.4 %fusion.55 = (f32[16384,128]{1,0:T(8,128)S(1)}, f32[16384,128]{1,0:T(8,128)S(1)}, f32[16384,128]{1,0:T(8,128)}, f32[16384,128]{1,0:T(8,128)}) fusion(s32[128]{0:T(128)S(1)} %get-tuple-element.178, s32[16384]{0:T(1024)S(1)} %add_select_fusion.5, s32[128]{0:T(128)S(1)} %get-tuple-element.179), kind=kLoop, calls=%fused_computation.27.clone.1 | loop fusion | flops 58720256 | bytes 33620992 | tf_op jit(solution)/shard_map/while/body/eval_jaxpr/cos | solution.py:24
  119.5 8.9 %fusion.58 = f32[8,256]{1,0:T(8,128)S(1)} fusion(bf16[8,16384]{1,0:T(8,128)(2,1)S(1)} %reshape.66, f32[16384,128]{1,0:T(8,128)} %get-tuple-element.184, f32[16384,128]{1,0:T(8,128)} %get-tuple-element.185), kind=kOutput, calls=%fused_computation.4.clone.1 | convolution fusion | flops 406847488 | bytes 17047552 | tf_op jit(solution)/shard_map/while/body/eval_jaxpr/dot_general | solution.py:34
  128.5 5.5 %fusion.56 = f32[8,256]{1,0:T(8,128)S(1)} fusion(bf16[8,16384]{1,0:T(8,128)(2,1)S(1)} %reshape.66, f32[16384,128]{1,0:T(8,128)S(1)} %get-tuple-element.180, f32[16384,128]{1,0:T(8,128)S(1)} %get-tuple-element.181), kind=kOutput, calls=%fused_computation.clone.1 | convolution fusion | flops 406847488 | bytes 17047552 | tf_op jit(solution)/shard_map/while/body/eval_jaxpr/dot_general | solution.py:34
  134.1 0.6 dynamic_slice.18
  136.6 0.1 constant_dynamic-slice_fusion.2
  136.7 0.1 reshape.66
  137.4 67.4 %fusion.55 = (f32[16384,128]{1,0:T(8,128)S(1)}, f32[16384,128]{1,0:T(8,128)S(1)}, f32[16384,128]{1,0:T(8,128)}, f32[16384,128]{1,0:T(8,128)}) fusion(s32[128]{0:T(128)S(1)} %get-tuple-element.178, s32[16384]{0:T(1024)S(1)} %add_select_fusion.5, s32[128]{0:T(128)S(1)} %get-tuple-element.179), kind=kLoop, calls=%fused_computation.27.clone.1 | loop fusion | flops 58720256 | bytes 33620992 | tf_op jit(solution)/shard_map/while/body/eval_jaxpr/cos | solution.py:24
  204.9 8.9 %fusion.58 = f32[8,256]{1,0:T(8,128)S(1)} fusion(bf16[8,16384]{1,0:T(8,128)(2,1)S(1)} %reshape.66, f32[16384,128]{1,0:T(8,128)} %get-tuple-element.184, f32[16384,128]{1,0:T(8,128)} %get-tuple-element.185), kind=kOutput, calls=%fused_computation.4.clone.1 | convolution fusion | flops 406847488 | bytes 17047552 | tf_op jit(solution)/shard_map/while/body/eval_jaxpr/dot_general | solution.py:34
  213.8 5.5 %fusion.56 = f32[8,256]{1,0:T(8,128)S(1)} fusion(bf16[8,16384]{1,0:T(8,128)(2,1)S(1)} %reshape.66, f32[16384,128]{1,0:T(8,128)S(1)} %get-tuple-element.180, f32[16384,128]{1,0:T(8,128)S(1)} %get-tuple-element.181), kind=kOutput, calls=%fused_computation.clone.1 | convolution fusion | flops 406847488 | bytes 17047552 | tf_op jit(solution)/shard_map/while/body/eval_jaxpr/dot_general | solution.py:34
  219.4 0.6 dynamic_slice.18
  221.9 0.1 constant_dynamic-slice_fusion.2
  222.0 0.1 reshape.66
  222.8 67.4 %fusion.55 = (f32[16384,128]{1,0:T(8,128)S(1)}, f32[16384,128]{1,0:T(8,128)S(1)}, f32[16384,128]{1,0:T(8,128)}, f32[16384,128]{1,0:T(8,128)}) fusion(s32[128]{0:T(128)S(1)} %get-tuple-element.178, s32[16384]{0:T(1024)S(1)} %add_select_fusion.5, s32[128]{0:T(128)S(1)} %get-tuple-element.179), kind=kLoop, calls=%fused_computation.27.clone.1 | loop fusion | flops 58720256 | bytes 33620992 | tf_op jit(solution)/shard_map/while/body/eval_jaxpr/cos | solution.py:24
  290.2 8.9 %fusion.58 = f32[8,256]{1,0:T(8,128)S(1)} fusion(bf16[8,16384]{1,0:T(8,128)(2,1)S(1)} %reshape.66, f32[16384,128]{1,0:T(8,128)} %get-tuple-element.184, f32[16384,128]{1,0:T(8,128)} %get-tuple-element.185), kind=kOutput, calls=%fused_computation.4.clone.1 | convolution fusion | flops 406847488 | bytes 17047552 | tf_op jit(solution)/shard_map/while/body/eval_jaxpr/dot_general | solution.py:34
  299.1 5.5 %fusion.56 = f32[8,256]{1,0:T(8,128)S(1)} fusion(bf16[8,16384]{1,0:T(8,128)(2,1)S(1)} %reshape.66, f32[16384,128]{1,0:T(8,128)S(1)} %get-tuple-element.180, f32[16384,128]{1,0:T(8,128)S(1)} %get-tuple-element.181), kind=kOutput, calls=%fused_computation.clone.1 | convolution fusion | flops 406847488 | bytes 17047552 | tf_op jit(solution)/shard_map/while/body/eval_jaxpr/dot_general | solution.py:34
  304.7 0.0 copy-start.2
  304.8 0.8 copy.13
  305.6 0.0 reduce-scatter.4.cloned.1.call-update
  305.6 56.0 %reduce-scatter.4.cloned.1.call-done = f32[16,4]{1,0:T(8,128)} async-done(((f32[256,4]{1,0:T(8,128)}), f32[16,4]{1,0:T(8,128)}) %reduce-scatter.4.cloned.1.call-update) | async-done | bytes 272
  361.6 1.3 copy.14
  362.9 0.0 copy-done.2
  (22 shorter events, 0.3 us)
Async XLA Ops:
  8.8 39.7 %copy-start = (s32[16384]{0:T(1024)S(1)}, s32[16384]{0:T(1024)}, u32[]{:S(2)}) copy-start(s32[16384]{0:T(1024)} %param.6) | copy-start | bytes 196612
  8.8 39.7 %copy-start.1 = (s32[256]{0:T(256)S(1)}, s32[256]{0:T(256)}, u32[]{:S(2)}) copy-start(s32[256]{0:T(256)} %param.7) | copy-start | bytes 3076
  21.4 26.1 %all-to-all-start = ((bf16[2,48,4,1024]{3,2,0,1:T(4,128)(2,1)}), bf16[2,48,4,1024]{3,2,0,1:T(4,128)(2,1)S(1)}, u32[]{:S(2)}, u32[]{:S(2)}) async-start(bf16[2,48,4,1024]{3,2,0,1:T(4,128)(2,1)} %copy.9), calls=%async_computation | async-start | bytes 1572864 | tf_op jit(solution)/shard_map/all_to_all | solution.py:58
  28.8 332.8 %reduce-scatter.4.cloned.1.call-start = ((), (), s32[]{:S(2)}) async-start(), calls=%async_computation.2 | async-start | bytes 139264
  304.7 58.2 %copy-start.2 = (f32[3,2,4,256]{3,2,1,0:T(4,128)}, f32[3,2,4,256]{3,2,1,0:T(4,128)S(1)}, u32[]{:S(2)}) copy-start(f32[3,2,4,256]{3,2,1,0:T(4,128)S(1)} %get-tuple-element.90) | copy-start | bytes 73732
Sparse Core Ops, SparseCore 0:
  305.7 55.8 reduce-scatter.3
where the time goes:
time: 370 us
  other arithmetic  204 us (55%)
  waiting for transfers between devices  74.7 us (20%)
  matrix products  54.4 us (15%)
  between operations  14.1 us (4%)
  loops' own time  7.92 us (2%)
  starting transfers between devices  7.43 us (2%)
  local copies, waits for them, and re-layouts  7.09 us (2%)
    cos x3, other arithmetic, make_phases(): return jnp.concatenate([jnp.cos(angles), jnp.sin(angles)], axis=1)  202 us
    unnamed x2, waiting for transfers between devices  56 us
    dot_general x6, matrix products, dedisperse(): jnp.dot(rows_wide, phases, precision=lax.Precision.HIGHEST, preferred_ele...  43.3 us
    all_to_all x1, waiting for transfers between devices, per_device(): lax.all_to_all(spectrum, 'chan', split_axis=1, concat_axis=3, tiled=True)  18.6 us
    dot_general x1, matrix products, per_device(): lax.dot_general(dft_table, voltages, (((0,), (2,)), ((), ())), preferred_...  11.1 us
    another operation x1, loops' own time, per_device(): spectra = lax.map(one_bin, jnp.arange(SPIN_DEV, dtype=jnp.int32))  7.92 us
  transfers between devices with their start and end apart: 2, of which 2 were waited for; matrix products, arithmetic and copies ran while one was open for 0% of the time, Pallas kernels for 0%

commit v1 on v0

v1 whole, which is shorter than its diff:
```python
import math

import jax
import jax.numpy as jnp
import numpy as np
from jax import lax
from jax.experimental import pallas as pl
from jax.experimental.pallas import tpu as pltpu
from jax.sharding import PartitionSpec as P

SUBSTEPS = 512
SPIN_DEV = 3
BLOCK = 256
LANES = 128
F32 = jnp.float32
BF16 = jnp.bfloat16

N_ALPHA = 8
N_A = 8
N_B = 4


def dft_rows(samples, bins):
    times = np.arange(samples, dtype=np.int64)
    freq = np.arange(bins, dtype=np.int64)
    angle = (freq[:, None] * times[None, :] % samples).astype(np.float32) * np.float32(
        2.0 * math.pi / samples
    )
    table = np.concatenate([np.cos(angle), -np.sin(angle)], axis=0)
    return table.astype(jnp.bfloat16)


def sign_matrix():
    out = np.zeros((128, 256), np.float32)
    for lane in range(128):
        a = lane // 8 - 7.5
        b = lane % 8 - 3.5
        sa, sb = np.sign(a), np.sign(b)
        j, k = int(abs(a) - 0.5), int(abs(b) - 0.5)
        col = lambda tb, ta: k * 32 + (tb * 2 + ta) * 8 + j
        out[col(0, 0), lane] = 1.0
        out[col(1, 1), lane] = -sa * sb
        out[col(0, 1), 128 + lane] = sa
        out[col(1, 0), 128 + lane] = sb
    return np.concatenate([out, out], axis=0).astype(jnp.bfloat16)


def cos_sin(phase, modulus):
    quarter = modulus // 4
    phase = phase & (modulus - 1)
    turn = lax.shift_right_logical(phase + quarter // 2, int(math.log2(quarter)))
    rest = phase - turn * quarter
    x = rest.astype(F32) * (2.0 * math.pi / modulus)
    z = x * x
    s = x + x * z * (-1.6666654611e-1 + z * (8.3321608736e-3 - z * 1.9515295891e-4))
    c = 1.0 - 0.5 * z + z * z * (
        4.166664568298827e-2 + z * (-1.388731625493765e-3 + z * 2.443315711809948e-5)
    )
    turn = turn & 3
    odd = (turn & 1) == 1
    cos_out = jnp.where(odd, s, c)
    sin_out = jnp.where(odd, c, s)
    cos_out = jnp.where((turn == 1) | (turn == 2), -cos_out, cos_out)
    sin_out = jnp.where(turn >= 2, -sin_out, sin_out)
    return cos_out, sin_out


def phase_kernel(
    bins,
    beams,
    groups,
    delay_ref,
    trials_ref,
    table_ref,
    signs_ref,
    volt_ref,
    keep_ref,
    send_ref,
    x_ref,
    acc_ref,
    sel_ref,
    mix_ref,
):
    step = pl.program_id(0)
    steps = pl.num_programs(0)
    samples = volt_ref.shape[2]
    block = volt_ref.shape[1]
    modulus = 2 * samples * SUBSTEPS
    tiles = block // LANES
    rows8 = 2 * beams

    @pl.when(step == 0)
    def _():
        acc_ref[...] = jnp.zeros_like(acc_ref)

    scale = 1.0 / math.sqrt(samples)
    for beam in range(beams):
        part = lax.dot_general(
            table_ref[...], volt_ref[beam], (((1,), (1,)), ((), ())), preferred_element_type=F32
        )
        part = (part * scale).astype(BF16).astype(F32)
        for k in range(2):
            for t in range(tiles):
                x_ref[t, pl.ds(k * beams + beam, bins, stride=rows8), :] = part[
                    k * bins : (k + 1) * bins, t * LANES : (t + 1) * LANES
                ]

    first = (lax.axis_index("chan") * steps + step) * tiles
    delay = jnp.concatenate([delay_ref[pl.ds(first + t, 1), :] for t in range(tiles)], axis=1)
    delay = jnp.broadcast_to(delay, (8, block))
    sub = lax.broadcasted_iota(jnp.int32, (8, block), 0)
    ca1, sa1 = cos_sin(delay * (128 * (2 * sub + 1)), modulus)
    cj1, sj1 = cos_sin(delay * (8 * (2 * sub + 1)), modulus)
    mult = jnp.where(sub < N_B, 2 * sub + 1, samples - 1)
    cb1, sb1 = cos_sin(delay * mult, modulus)

    def turn(c, s, c1, s1):
        return c * c1 - s * s1, c * s1 + s * c1

    sign = jnp.where(sub < beams, -1.0, 1.0).astype(F32)

    def row(x, r):
        return jnp.broadcast_to(x[r : r + 1, :], (8, block))

    def one_bin(f, carry):
        ca, sa, cj, sj, cb, sb = carry
        base = pl.multiple_of(f * rows8, rows8)
        x = jnp.concatenate([x_ref[t, pl.ds(base, rows8), :] for t in range(tiles)], axis=1)
        z = x * row(cb, N_B) + pltpu.roll(x, beams, 0) * (sign * row(sb, N_B))
        lhs = []
        for r in range(rows8):
            zr = row(z, r)
            lhs += [zr * ca, zr * sa]
        rhs = []
        for k in range(N_B):
            c, s = row(cb, k), row(sb, k)
            rhs += [c * cj, c * sj, s * cj, s * sj]
        lhs = jnp.concatenate(lhs, axis=0).astype(BF16)
        rhs = jnp.concatenate(rhs, axis=0).astype(BF16)
        acc_ref[f] += lax.dot_general(
            lhs, rhs, (((1,), (1,)), ((), ())), preferred_element_type=F32
        )
        ca, sa = turn(ca, sa, ca1, sa1)
        cj, sj = turn(cj, sj, cj1, sj1)
        cb, sb = turn(cb, sb, cb1, sb1)
        return ca, sa, cj, sj, cb, sb

    one = jnp.ones((8, block), F32)
    zero = jnp.zeros((8, block), F32)
    lax.fori_loop(0, bins, one_bin, (one, zero, one, zero, one, zero), unroll=4)

    @pl.when(step == steps - 1)
    def _():
        half = beams * 8

        def mix(f, carry):
            g = acc_ref[f]
            plus, minus = [], []
            for b in range(beams):
                zc = g[b * 16 : b * 16 + 8]
                zs = g[b * 16 + 8 : b * 16 + 16]
                wc = g[(beams + b) * 16 : (beams + b) * 16 + 8]
                ws = g[(beams + b) * 16 + 8 : (beams + b) * 16 + 16]
                plus.append((zc - ws, zs + wc))
                minus.append((zc + ws, wc - zs))
            q = jnp.concatenate(
                [p[0] for p in plus]
                + [p[0] for p in minus]
                + [p[1] for p in plus]
                + [p[1] for p in minus],
                axis=0,
            )
            hi = q.astype(BF16)
            lo = (q - hi.astype(F32)).astype(BF16)
            u = jnp.dot(
                jnp.concatenate([hi, lo], axis=1), signs_ref[...], preferred_element_type=F32
            )
            re = u[: 2 * half, :128] - u[2 * half :, 128:]
            im = u[: 2 * half, 128:] + u[2 * half :, :128]
            base = pl.multiple_of(f * 2 * half, half)
            for s in range(2):
                sel_ref[s, pl.ds(base, half), :] = re[s * half : (s + 1) * half]
                sel_ref[s, pl.ds(base + half, half), :] = im[s * half : (s + 1) * half]
            return carry

        lax.fori_loop(0, bins, mix, 0, unroll=4)

        rows = bins * rows8
        trials = trials_ref[...]
        count = trials.shape[1]
        lane = lax.broadcasted_iota(jnp.int32, (128, count), 0)
        total = jnp.zeros((rows, count), F32)
        for s in range(2):
            for a in range(N_ALPHA):
                low = samples // 2 + 128 * a if s == 0 else samples // 2 - 128 * (a + 1)
                pick = (lane + low == trials).astype(F32).astype(BF16)
                y = sel_ref[s, pl.ds(a, rows, stride=8), :]
                hi = y.astype(BF16)
                lo = (y - hi.astype(F32)).astype(BF16)
                total += jnp.dot(
                    jnp.concatenate([hi, lo], axis=1),
                    jnp.concatenate([pick, pick], axis=0),
                    preferred_element_type=F32,
                )
        flip = total.T
        per = rows // groups
        tper = count // groups
        bins_rows = per * (count // LANES)
        for g in range(groups):
            for h in range(count // LANES):
                mix_ref[g % 2, g // 2, h * per : (h + 1) * per, :] = total[
                    g * per : (g + 1) * per, h * LANES : (h + 1) * LANES
                ]
            for m in range(rows // LANES):
                mix_ref[
                    g % 2, g // 2, bins_rows + m * tper : bins_rows + (m + 1) * tper, :
                ] = flip[g * tper : (g + 1) * tper, m * LANES : (m + 1) * LANES]
        mine = lax.rem(lax.axis_index("chan"), 2)
        keep_ref[...] = mix_ref[mine]
        send_ref[...] = mix_ref[1 - mine]


def per_device(voltages, delay_step, trials):
    beams, local_chan, samples = voltages.shape
    groups = lax.axis_size("chan")
    bins = SPIN_DEV * groups
    all_chan = delay_step.shape[0]
    count = trials.shape[0]
    chan_scale = 1.0 / math.sqrt(all_chan)
    block = min(BLOCK, local_chan)
    steps = local_chan // block
    tiles = block // LANES
    rows8 = 2 * beams
    rows = bins * rows8
    per = rows // groups
    tper = count // groups
    bins_rows = per * (count // LANES)
    out_rows = bins_rows + tper * (rows // LANES)

    table = jnp.asarray(dft_rows(samples, bins))
    signs = jnp.asarray(sign_matrix())
    full = lambda *shape: pl.BlockSpec(shape, lambda i: (0,) * len(shape))
    piece = jax.ShapeDtypeStruct((groups // 2, out_rows, LANES), F32)
    keep, send = pl.pallas_call(
        lambda *refs: phase_kernel(bins, beams, groups, *refs),
        grid=(steps,),
        in_specs=[
            full(all_chan // LANES, LANES),
            full(1, count),
            full(2 * bins, samples),
            full(256, 256),
            pl.BlockSpec((beams, block, samples), lambda i: (0, i, 0)),
        ],
        out_specs=[full(*piece.shape), full(*piece.shape)],
        out_shape=[piece, piece],
        scratch_shapes=[
            pltpu.VMEM((tiles, rows, LANES), F32),
            pltpu.VMEM((bins, 16 * rows8, 128), F32),
            pltpu.VMEM((2, rows * 8, 128), F32),
            pltpu.VMEM((2, groups // 2, out_rows, LANES), F32),
        ],
        compiler_params=pltpu.CompilerParams(
            dimension_semantics=("arbitrary",), vmem_limit_bytes=60 << 20
        ),
        name="dedisperse",
    )(
        delay_step.reshape(-1, LANES),
        trials.reshape(1, count),
        table,
        signs,
        voltages,
    )

    index = lax.axis_index("chan")
    received = lax.ppermute(send, "chan", [(i, i ^ 1) for i in range(groups)])
    own = keep + received
    bit = 2
    while bit < groups:
        own = own.reshape(-1, 2, out_rows, LANES)
        mine = (index // bit) % 2
        other = lax.dynamic_index_in_dim(own, 1 - mine, 1, keepdims=False)
        if bit == 2:
            other = other.astype(BF16)
        received = lax.ppermute(other, "chan", [(i, i ^ bit) for i in range(groups)])
        own = lax.dynamic_index_in_dim(own, mine, 1, keepdims=False) + received.astype(F32)
        bit *= 2
    own = own.reshape(out_rows, LANES) * chan_scale
    spectra = own[:bins_rows].reshape(count // LANES, per, LANES).transpose(1, 0, 2)
    spectra = spectra.reshape(SPIN_DEV, 2, beams, count)
    square = own[bins_rows:]
    square = square * square
    square = square.reshape(-1, tper, LANES // beams, beams)
    power = jnp.sum(square, axis=(0, 2)).T / bins
    return spectra, power


def solution(mesh):
    return jax.shard_map(
        per_device,
        mesh=mesh,
        in_specs=(P("grp", "chan", None), P(), P()),
        out_specs=(P("chan", None, "grp", None), P("grp", "chan")),
        check_vma=False,
    )
```

time: 370 us -> 46.9 us (0.13)
  other arithmetic: 204 us -> 1.75 us
  waiting for transfers between devices: 74.7 us -> 9.63 us
  matrix products: 54.4 us -> 0 us
  Pallas kernels: 0 us -> 25.5 us
  between operations: 14.1 us -> 0.7 us
  loops' own time: 7.92 us -> 0 us
  local copies, waits for them, and re-layouts: 7.09 us -> 0.95 us
    cos x3 -> x0, other arithmetic: 202 us -> none  [make_phases(): return jnp.concatenate([jnp.cos(angles), jnp.sin(angles)], axis=1)]
    unnamed x2 -> x0, waiting for transfers between devices: 56 us -> none
    dot_general x7 -> x0, matrix products: 54.4 us -> none  [the longest x6 43.3 us: dedisperse(): jnp.dot(rows_wide, phases, precision=lax.Precision.HIGHEST, preferred_ele...]
    pallas_call x0 -> x1, Pallas kernels: none -> 25.5 us  [per_device(): pl.pallas_call(lambda *refs: phase_kernel(bins, beams, groups, *refs), gr...]
    all_to_all x1 -> x0, waiting for transfers between devices: 18.6 us -> none  [per_device(): lax.all_to_all(spectrum, 'chan', split_axis=1, concat_axis=3, tiled=True)]
    ppermute x0 -> x4, waiting for transfers between devices: none -> 9.63 us  [the longest x3 8.07 us: per_device(): lax.ppermute(other, 'chan', [(i, i ^ bit) for i in range(groups)])]
    ppermute x0 -> x4, starting transfers between devices: none -> 8.17 us  [the longest x3 7.71 us: per_device(): lax.ppermute(other, 'chan', [(i, i ^ bit) for i in range(groups)])]
    another operation x1 -> x0, loops' own time: 7.92 us -> none  [per_device(): spectra = lax.map(one_bin, jnp.arange(SPIN_DEV, dtype=jnp.int32))]
  transfers between devices with their start and end apart: 2 -> 4, of which waited for: 2 -> 4; matrix products, arithmetic and copies ran while one was open for 0% -> 0% of each run, Pallas kernels for 0% -> 0%
where the time goes in v1:
time: 46.9 us; the launch traced here: 46.7 us
  Pallas kernels  25.5 us (54%)
  waiting for transfers between devices  9.63 us (21%)
  starting transfers between devices  8.17 us (17%)
  other arithmetic  1.75 us (4%)
  local copies, waits for them, and re-layouts  0.95 us (2%)
  between operations  0.7 us (1%)
    pallas_call x1, Pallas kernels, per_device(): pl.pallas_call(lambda *refs: phase_kernel(bins, beams, groups, *refs), gr...  25.5 us
    ppermute x3, waiting for transfers between devices, per_device(): lax.ppermute(other, 'chan', [(i, i ^ bit) for i in range(groups)])  8.07 us
    ppermute x3, starting transfers between devices, per_device(): lax.ppermute(other, 'chan', [(i, i ^ bit) for i in range(groups)])  7.71 us
    ppermute x1, waiting for transfers between devices, per_device(): received = lax.ppermute(send, 'chan', [(i, i ^ 1) for i in range(groups)])  1.56 us
    add x1, other arithmetic, per_device(): own = keep + received  1.04 us
  transfers between devices with their start and end apart: 4, of which 4 were waited for; matrix products, arithmetic and copies ran while one was open for 0% of the time, Pallas kernels for 0%

profile of v1, /device:TPU:0, one launch (start us, length us, event | category | flops | bytes accessed | tf_op | source)
XLA Modules:
  0.0 46.7 jit_solution(11364524263028332513)
XLA Ops:
  0.6 25.5 %dedisperse.1 = (f32[8,96,128]{2,1,0:T(8,128)}, f32[8,96,128]{2,1,0:T(8,128)}) custom-call(s32[128,128]{1,0:T(8,128)} %bitcast.28, s32[1,256]{1,0:T(1,128)} %bitcast.29, bf16[96,2048]{1,0:T(8,128)(2,1)} %constant.89.clone.refs_2_, bf16[256,256]{1,0:T(8,128)(2,1)} %constant.90.clone.refs_3_, bf16[4,1024,2048]{2,1,0:T(8,128)(2,1)} %refs_4_.1), custom_call_target="tpu_custom_call" | custom-call | tf_op jit(solution)/shard_map/dedisperse/pallas_call | solution.py:244
  26.2 0.5 collective-permute-start
  26.6 1.6 %collective-permute-done = f32[8,96,128]{2,1,0:T(8,128)S(1)} collective-permute-done((f32[8,96,128]{2,1,0:T(8,128)}, f32[8,96,128]{2,1,0:T(8,128)S(1)}, u32[]{:S(2)}, u32[]{:S(2)}) %collective-permute-start) | collective-permute-done | bytes 393248 | tf_op jit(solution)/shard_map/ppermute | solution.py:275
  28.2 1.0 %add.49 = f32[8,96,128]{2,1,0:T(8,128)S(1)} add(f32[8,96,128]{2,1,0:T(8,128)} %get-tuple-element.4, f32[8,96,128]{2,1,0:T(8,128)S(1)} %collective-permute-done) | non-fusion elementwise | flops 98304 | bytes 1179648 | tf_op jit(solution)/shard_map/add | solution.py:276
  29.3 2.9 %collective-permute-start.1 = (bf16[4,96,128]{2,1,0:T(8,128)(2,1)S(1)}, bf16[4,96,128]{2,1,0:T(8,128)(2,1)S(1)}, u32[]{:S(2)}, u32[]{:S(2)}) collective-permute-start(bf16[4,96,128]{2,1,0:T(8,128)(2,1)S(1)} %fusion), channel_id=1, source_target_pairs={{0,2},{1,3},{2,0},{3,1},{4,6},{5,7},{6,4},{7,5},{8,10},{9,11},{10,... | collective-permute-start | bytes 294920 | tf_op jit(solution)/shard_map/ppermute | solution.py:284
  32.2 3.1 %collective-permute-done.1 = bf16[4,96,128]{2,1,0:T(8,128)(2,1)S(1)} collective-permute-done((bf16[4,96,128]{2,1,0:T(8,128)(2,1)S(1)}, bf16[4,96,128]{2,1,0:T(8,128)(2,1)S(1)}, u32[]{:S(2)}, u32[]{:S(2)}) %collective-permute-start.1) | collective-permute-done | bytes 98336 | tf_op jit(solution)/shard_map/ppermute | solution.py:284
  35.4 1.9 %collective-permute-start.2 = (f32[2,96,128]{2,1,0:T(8,128)S(1)}, f32[2,96,128]{2,1,0:T(8,128)S(1)}, u32[]{:S(2)}, u32[]{:S(2)}) collective-permute-start(f32[2,96,128]{2,1,0:T(8,128)S(1)} %dynamic-slice_bitcast_fusion), channel_id=1, source_target_pairs={{0,4},{1,5},{2,6},{3,7},{4,0},{5,1},{6,2},{7,3},{8,12},{9,13},{10,... | collective-permute-start | bytes 294920 | tf_op jit(solution)/shard_map/ppermute | solution.py:284
  37.2 2.8 %collective-permute-done.2 = f32[2,96,128]{2,1,0:T(8,128)S(1)} collective-permute-done((f32[2,96,128]{2,1,0:T(8,128)S(1)}, f32[2,96,128]{2,1,0:T(8,128)S(1)}, u32[]{:S(2)}, u32[]{:S(2)}) %collective-permute-start.2) | collective-permute-done | bytes 98336 | tf_op jit(solution)/shard_map/ppermute | solution.py:284
  40.1 2.9 %collective-permute-start.3 = (f32[1,96,128]{2,1,0:T(8,128)S(1)}, f32[1,96,128]{2,1,0:T(8,128)S(1)}, u32[]{:S(2)}, u32[]{:S(2)}) collective-permute-start(f32[1,96,128]{2,1,0:T(8,128)S(1)} %constant_dynamic-slice_fusion), channel_id=1, source_target_pairs={{0,8},{1,9},{2,10},{3,11},{4,12},{5,13},{6,14},{7,15},{8,0},{9,1},... | collective-permute-start | bytes 147464 | tf_op jit(solution)/shard_map/ppermute | solution.py:284
  43.0 2.2 %collective-permute-done.3 = f32[1,96,128]{2,1,0:T(8,128)S(1)} collective-permute-done((f32[1,96,128]{2,1,0:T(8,128)S(1)}, f32[1,96,128]{2,1,0:T(8,128)S(1)}, u32[]{:S(2)}, u32[]{:S(2)}) %collective-permute-start.3) | collective-permute-done | bytes 49184 | tf_op jit(solution)/shard_map/ppermute | solution.py:284
  45.2 0.6 %reshape.44 = f32[3,2,4,256]{3,2,1,0:T(4,128)} reshape(f32[24,2,128]{2,1,0:T(2,128)S(1)} %copy.12) | data formatting | bytes 49152 | tf_op jit(solution)/shard_map/reshape | solution.py:289
  45.8 0.1 copy.13
  45.9 0.2 reshape.45
  46.1 0.1 reduce_sum.9
  46.2 0.6 %multiply_bitcast_fusion = f32[4,16]{1,0:T(4,128)} fusion(f32[16,4]{0,1:T(4,128)S(1)} %reduce_sum.9), kind=kLoop, calls=%fused_computation.7 | loop fusion | flops 64 | bytes 512 | tf_op jit(solution)/shard_map/div | solution.py:293
  (8 shorter events, 0.1 us)
Async XLA Ops:
  26.2 2.0 %collective-permute-start = (f32[8,96,128]{2,1,0:T(8,128)}, f32[8,96,128]{2,1,0:T(8,128)S(1)}, u32[]{:S(2)}, u32[]{:S(2)}) collective-permute-start(f32[8,96,128]{2,1,0:T(8,128)} %get-tuple-element.5), channel_id=1, source_target_pairs={{0,1},{1,0},{2,3},{3,2},{4,5},{5,4},{6,7},{7,6},{8,9},{9,8},{10,11... | collective-permute-start | bytes 1179656 | tf_op jit(solution)/shard_map/ppermute | solution.py:275
  29.3 6.0 %collective-permute-start.1 = (bf16[4,96,128]{2,1,0:T(8,128)(2,1)S(1)}, bf16[4,96,128]{2,1,0:T(8,128)(2,1)S(1)}, u32[]{:S(2)}, u32[]{:S(2)}) collective-permute-start(bf16[4,96,128]{2,1,0:T(8,128)(2,1)S(1)} %fusion), channel_id=1, source_target_pairs={{0,2},{1,3},{2,0},{3,1},{4,6},{5,7},{6,4},{7,5},{8,10},{9,11},{10,... | collective-permute-start | bytes 294920 | tf_op jit(solution)/shard_map/ppermute | solution.py:284
  35.4 4.7 %collective-permute-start.2 = (f32[2,96,128]{2,1,0:T(8,128)S(1)}, f32[2,96,128]{2,1,0:T(8,128)S(1)}, u32[]{:S(2)}, u32[]{:S(2)}) collective-permute-start(f32[2,96,128]{2,1,0:T(8,128)S(1)} %dynamic-slice_bitcast_fusion), channel_id=1, source_target_pairs={{0,4},{1,5},{2,6},{3,7},{4,0},{5,1},{6,2},{7,3},{8,12},{9,13},{10,... | collective-permute-start | bytes 294920 | tf_op jit(solution)/shard_map/ppermute | solution.py:284
  40.1 5.1 %collective-permute-start.3 = (f32[1,96,128]{2,1,0:T(8,128)S(1)}, f32[1,96,128]{2,1,0:T(8,128)S(1)}, u32[]{:S(2)}, u32[]{:S(2)}) collective-permute-start(f32[1,96,128]{2,1,0:T(8,128)S(1)} %constant_dynamic-slice_fusion), channel_id=1, source_target_pairs={{0,8},{1,9},{2,10},{3,11},{4,12},{5,13},{6,14},{7,15},{8,0},{9,1},... | collective-permute-start | bytes 147464 | tf_op jit(solution)/shard_map/ppermute | solution.py:284

commit v2 on v1

v2 whole, which is shorter than its diff:
```python
import math

import jax
import jax.numpy as jnp
import numpy as np
from jax import lax
from jax.experimental import pallas as pl
from jax.experimental.pallas import tpu as pltpu
from jax.sharding import PartitionSpec as P

SUBSTEPS = 512
SPIN_DEV = 3
BLOCK = 256
LANES = 128
F32 = jnp.float32
BF16 = jnp.bfloat16

N_ALPHA = 8
N_B = 4


def dft_rows(samples, bins):
    times = np.arange(samples, dtype=np.int64)
    freq = np.arange(bins, dtype=np.int64)
    angle = (freq[:, None] * times[None, :] % samples).astype(np.float32) * np.float32(
        2.0 * math.pi / samples
    )
    table = np.concatenate([np.cos(angle), -np.sin(angle)], axis=0)
    return table.astype(jnp.bfloat16)


def sign_matrix():
    out = np.zeros((128, 256), np.float32)
    for lane in range(128):
        a = lane // 8 - 7.5
        b = lane % 8 - 3.5
        sa, sb = np.sign(a), np.sign(b)
        j, k = int(abs(a) - 0.5), int(abs(b) - 0.5)
        col = lambda tb, ta: k * 32 + (tb * 2 + ta) * 8 + j
        out[col(0, 0), lane] = 1.0
        out[col(1, 1), lane] = -sa * sb
        out[col(0, 1), 128 + lane] = sa
        out[col(1, 0), 128 + lane] = sb
    return np.concatenate([out, out], axis=0).astype(jnp.bfloat16)


def cos_sin(phase, modulus):
    quarter = modulus // 4
    phase = phase & (modulus - 1)
    turn = lax.shift_right_logical(phase + quarter // 2, int(math.log2(quarter)))
    rest = phase - turn * quarter
    x = rest.astype(F32) * (2.0 * math.pi / modulus)
    z = x * x
    s = x + x * z * (-1.6666654611e-1 + z * (8.3321608736e-3 - z * 1.9515295891e-4))
    c = 1.0 - 0.5 * z + z * z * (
        4.166664568298827e-2 + z * (-1.388731625493765e-3 + z * 2.443315711809948e-5)
    )
    turn = turn & 3
    odd = (turn & 1) == 1
    cos_out = jnp.where(odd, s, c)
    sin_out = jnp.where(odd, c, s)
    cos_out = jnp.where((turn == 1) | (turn == 2), -cos_out, cos_out)
    sin_out = jnp.where(turn >= 2, -sin_out, sin_out)
    return cos_out, sin_out


def turned(c, s, c1, s1):
    return c * c1 - s * s1, c * s1 + s * c1


def phase_kernel(
    groups,
    delay_ref,
    trials_ref,
    table_ref,
    signs_ref,
    volt_ref,
    keep_ref,
    send_ref,
    new_x_ref,
    new_b_ref,
    x_ref,
    b_ref,
    one_ref,
    acc_ref,
    sel_ref,
    mix_ref,
):
    step = pl.program_id(0)
    steps = pl.num_programs(0) - 1
    beams, block, samples = volt_ref.shape
    bins = acc_ref.shape[0]
    modulus = 2 * samples * SUBSTEPS
    tiles = block // LANES
    rows8 = 2 * beams
    scale = 1.0 / math.sqrt(samples)

    def angles():
        first = (lax.axis_index("chan") * steps + step) * tiles
        delay = jnp.concatenate([delay_ref[pl.ds(first + t, 1), :] for t in range(tiles)], axis=1)
        delay = jnp.broadcast_to(delay, (8, block))
        sub = lax.broadcasted_iota(jnp.int32, (8, block), 0)
        one_ref[0], one_ref[1] = cos_sin(delay * (128 * (2 * sub + 1)), modulus)
        one_ref[2], one_ref[3] = cos_sin(delay * (8 * (2 * sub + 1)), modulus)

        def ladder(mult):
            c, s = cos_sin(delay * (mult * sub), modulus)
            c1, s1 = cos_sin(delay * (mult * 8), modulus)
            cs, ss = [c], [s]
            for _ in range(bins // 8 - 1):
                c, s = turned(c, s, c1, s1)
                cs.append(c)
                ss.append(s)
            return jnp.concatenate(cs, axis=0), jnp.concatenate(ss, axis=0)

        for k in range(N_B):
            c, s = ladder(2 * k + 1)
            for t in range(tiles):
                lanes = slice(t * LANES, (t + 1) * LANES)
                new_b_ref[t, 2 * k] = c[:, lanes]
                new_b_ref[t, 2 * k + 1] = s[:, lanes]
        return ladder(samples - 1)

    def spectrum(beam, middle):
        part = lax.dot_general(
            volt_ref[beam], table_ref[...], (((1,), (1,)), ((), ())), preferred_element_type=F32
        ).T
        part = (part * scale).astype(BF16).astype(F32)
        zr, zi = turned(part[:bins], part[bins:], *middle)
        for t in range(tiles):
            lanes = slice(t * LANES, (t + 1) * LANES)
            new_x_ref[t, beam] = zr[:, lanes]
            new_x_ref[t, beams + beam] = zi[:, lanes]

    def spread(ref, r, f):
        return jnp.concatenate(
            [jnp.broadcast_to(ref[t, r, pl.ds(f, 1), :], (8, LANES)) for t in range(tiles)], axis=1
        )

    def take():
        x_ref[...] = new_x_ref[...]
        b_ref[...] = new_b_ref[...]
        return tuple(one_ref[n] for n in range(4))

    def some_bins(quarter, carry, unit):
        ca1, sa1, cj1, sj1 = unit

        def one_bin(f, carry):
            ca, sa, cj, sj = carry
            lhs = []
            for r in range(rows8):
                zr = spread(x_ref, r, f)
                lhs += [zr * ca, zr * sa]
            rhs = []
            for k in range(N_B):
                c, s = spread(b_ref, 2 * k, f), spread(b_ref, 2 * k + 1, f)
                rhs += [c * cj, c * sj, s * cj, s * sj]
            lhs = jnp.concatenate(lhs, axis=0).astype(BF16)
            rhs = jnp.concatenate(rhs, axis=0).astype(BF16)
            acc_ref[f] += lax.dot_general(
                lhs, rhs, (((1,), (1,)), ((), ())), preferred_element_type=F32
            )
            ca, sa = turned(ca, sa, ca1, sa1)
            cj, sj = turned(cj, sj, cj1, sj1)
            return ca, sa, cj, sj

        size = bins // 4
        return lax.fori_loop(quarter * size, (quarter + 1) * size, one_bin, carry, unroll=12)

    one = jnp.ones((8, block), F32)
    zero = jnp.zeros((8, block), F32)
    start = (one, zero, one, zero)

    def last():
        half = beams * 8

        def mix(f, carry):
            g = acc_ref[f]
            plus, minus = [], []
            for b in range(beams):
                zc = g[b * 16 : b * 16 + 8]
                zs = g[b * 16 + 8 : b * 16 + 16]
                wc = g[(beams + b) * 16 : (beams + b) * 16 + 8]
                ws = g[(beams + b) * 16 + 8 : (beams + b) * 16 + 16]
                plus.append((zc - ws, zs + wc))
                minus.append((zc + ws, wc - zs))
            q = jnp.concatenate(
                [p[0] for p in plus]
                + [p[0] for p in minus]
                + [p[1] for p in plus]
                + [p[1] for p in minus],
                axis=0,
            )
            hi = q.astype(BF16)
            lo = (q - hi.astype(F32)).astype(BF16)
            u = jnp.dot(
                jnp.concatenate([hi, lo], axis=1), signs_ref[...], preferred_element_type=F32
            )
            re = u[: 2 * half, :128] - u[2 * half :, 128:]
            im = u[: 2 * half, 128:] + u[2 * half :, :128]
            base = pl.multiple_of(f * 2 * half, half)
            for s in range(2):
                sel_ref[s, pl.ds(base, half), :] = re[s * half : (s + 1) * half]
                sel_ref[s, pl.ds(base + half, half), :] = im[s * half : (s + 1) * half]
            return carry

        lax.fori_loop(0, bins, mix, 0, unroll=48)

        rows = bins * rows8
        trials = trials_ref[...]
        count = trials.shape[1]
        lane = lax.broadcasted_iota(jnp.int32, (128, count), 0)
        every, picks = [], []
        for s in range(2):
            for a in range(N_ALPHA):
                low = samples // 2 + 128 * a if s == 0 else samples // 2 - 128 * (a + 1)
                picks.append((lane + low == trials).astype(F32).astype(BF16))
                every.append(sel_ref[s, pl.ds(a, rows, stride=8), :].astype(BF16))
        total = jnp.dot(
            jnp.concatenate(every, axis=1),
            jnp.concatenate(picks, axis=0),
            preferred_element_type=F32,
        )
        flip = total.T
        per = rows // groups
        tper = count // groups
        for g in range(groups):
            piece = [
                total[g * per : (g + 1) * per, h * LANES : (h + 1) * LANES]
                for h in range(count // LANES)
            ] + [
                flip[g * tper : (g + 1) * tper, m * LANES : (m + 1) * LANES]
                for m in range(rows // LANES)
            ]
            mix_ref[g % 2, g // 2] = jnp.concatenate(piece, axis=0).astype(mix_ref.dtype)
        mine = lax.axis_index("chan") & 1
        keep_ref[...] = mix_ref[mine]
        send_ref[...] = mix_ref[1 - mine]

    @pl.when(step == 0)
    def _():
        acc_ref[...] = jnp.zeros_like(acc_ref)
        middle = angles()
        for beam in range(beams):
            spectrum(beam, middle)

    @pl.when((step > 0) & (step < steps))
    def _():
        unit = take()
        middle = angles()
        turn = start
        for quarter in range(4):
            for beam in range(beams * quarter // 4, beams * (quarter + 1) // 4):
                spectrum(beam, middle)
            turn = some_bins(quarter, turn, unit)

    @pl.when(step == steps)
    def _():
        unit = take()
        turn = start
        for quarter in range(4):
            turn = some_bins(quarter, turn, unit)
        last()


def finish_kernel(bins, chan_scale, own_ref, received_ref, spectra_ref, power_ref):
    spin, _, beams, count = spectra_ref.shape
    tper = power_ref.shape[1]
    rows = bins * 2 * beams
    per = spin * 2 * beams
    half = lax.axis_size("chan") // 2
    mine = (lax.axis_index("chan") & half) // half
    total = (own_ref[mine] + received_ref[...]) * chan_scale
    for h in range(count // LANES):
        for f in range(spin):
            for k in range(2):
                row = h * per + (f * 2 + k) * beams
                spectra_ref[f, k, :, h * LANES : (h + 1) * LANES] = total[row : row + beams]
    first = per * (count // LANES)
    power = jnp.zeros((tper, LANES), F32)
    for m in range(rows // LANES):
        part = total[first + m * tper : first + (m + 1) * tper]
        power += part * part
    beam_of = lax.broadcasted_iota(jnp.int32, (8, LANES), 1) % beams
    pick = (beam_of == lax.broadcasted_iota(jnp.int32, (8, LANES), 0)).astype(F32)
    power = lax.dot_general(
        pick,
        power,
        (((1,), (1,)), ((), ())),
        precision=lax.Precision.HIGHEST,
        preferred_element_type=F32,
    )
    power_ref[...] = power[:beams] / bins


def per_device(voltages, delay_step, trials):
    beams, local_chan, samples = voltages.shape
    groups = lax.axis_size("chan")
    bins = SPIN_DEV * groups
    all_chan = delay_step.shape[0]
    count = trials.shape[0]
    block = min(BLOCK, local_chan)
    steps = local_chan // block
    tiles = block // LANES
    rows8 = 2 * beams
    rows = bins * rows8
    per = rows // groups
    tper = count // groups
    out_rows = per * (count // LANES) + tper * (rows // LANES)

    full = lambda *shape: pl.BlockSpec(shape, lambda i: (0,) * len(shape))
    vmem = pl.BlockSpec(memory_space=pltpu.VMEM)
    piece = jax.ShapeDtypeStruct((groups // 2, out_rows, LANES), BF16)
    keep, send = pl.pallas_call(
        lambda *refs: phase_kernel(groups, *refs),
        grid=(steps + 1,),
        in_specs=[
            full(all_chan // LANES, LANES),
            full(1, count),
            full(2 * bins, samples),
            full(256, 256),
            pl.BlockSpec(
                (beams, block, samples), lambda i: (0, jnp.minimum(i, steps - 1), 0)
            ),
        ],
        out_specs=[full(*piece.shape), full(*piece.shape)],
        out_shape=[piece, piece],
        scratch_shapes=[
            pltpu.VMEM((tiles, rows8, bins, LANES), F32),
            pltpu.VMEM((tiles, 2 * N_B, bins, LANES), F32),
            pltpu.VMEM((tiles, rows8, bins, LANES), F32),
            pltpu.VMEM((tiles, 2 * N_B, bins, LANES), F32),
            pltpu.VMEM((4, 8, block), F32),
            pltpu.VMEM((bins, 16 * rows8, 128), F32),
            pltpu.VMEM((2, rows * 8, 128), F32),
            pltpu.VMEM((2, groups // 2, out_rows, LANES), BF16),
        ],
        compiler_params=pltpu.CompilerParams(
            dimension_semantics=("arbitrary",), vmem_limit_bytes=60 << 20
        ),
        name="dedisperse",
    )(
        delay_step.reshape(-1, LANES),
        trials.reshape(1, count),
        jnp.asarray(dft_rows(samples, bins)),
        jnp.asarray(sign_matrix()),
        voltages,
    )

    index = lax.axis_index("chan")
    received = lax.ppermute(send, "chan", [(i, i ^ 1) for i in range(groups)])
    own = keep.astype(F32) + received.astype(F32)
    bit = 2
    while True:
        own = own.reshape(-1, 2, out_rows, LANES)
        mine = (index & bit) // bit
        other = lax.dynamic_index_in_dim(own, 1 - mine, 1, keepdims=False)
        if bit == 2:
            other = other.astype(BF16)
        received = lax.ppermute(other, "chan", [(i, i ^ bit) for i in range(groups)])
        if 2 * bit == groups:
            break
        own = lax.dynamic_index_in_dim(own, mine, 1, keepdims=False) + received.astype(F32)
        bit *= 2
    return pl.pallas_call(
        lambda *refs: finish_kernel(bins, 1.0 / math.sqrt(all_chan), *refs),
        in_specs=[vmem, vmem],
        out_specs=[vmem, vmem],
        out_shape=[
            jax.ShapeDtypeStruct((SPIN_DEV, 2, beams, count), F32),
            jax.ShapeDtypeStruct((beams, tper), F32),
        ],
        compiler_params=pltpu.CompilerParams(vmem_limit_bytes=4 << 20),
        name="finish",
    )(own.reshape(2, out_rows, LANES), received.reshape(out_rows, LANES))


def solution(mesh):
    return jax.shard_map(
        per_device,
        mesh=mesh,
        in_specs=(P("grp", "chan", None), P(), P()),
        out_specs=(P("chan", None, "grp", None), P("grp", "chan")),
        check_vma=False,
    )
```

time: 46.9 us -> 34.3 us (0.73)
  Pallas kernels: 25.5 us -> 14.9 us
  local copies, waits for them, and re-layouts: 0.95 us -> 0.05 us
  other arithmetic: 1.75 us -> 1 us
    pallas_call x1 -> x2, Pallas kernels: 25.5 us -> 14.9 us  [the longest x1 14.2 us: per_device(): pl.pallas_call(lambda *refs: phase_kernel(groups, *refs), grid=(steps + 1...]
    reshape x2 -> x0, local copies, waits for them, and re-layouts: 0.79 us -> none  [the longest x1 0.63 us: per_device(): spectra = spectra.reshape(SPIN_DEV, 2, beams, count)]
    div x1 -> x0, other arithmetic: 0.58 us -> none  [per_device(): power = jnp.sum(square, axis=(0, 2)).T / bins]
where the time goes in v2:
time: 34.3 us; the launch traced here: 34.2 us
  Pallas kernels  14.9 us (43%)
  waiting for transfers between devices  9.37 us (27%)
  starting transfers between devices  8.14 us (24%)
  other arithmetic  1 us (3%)
  between operations  0.67 us (2%)
    pallas_call x1, Pallas kernels, per_device(): pl.pallas_call(lambda *refs: phase_kernel(groups, *refs), grid=(steps + 1...  14.2 us
    ppermute x3, waiting for transfers between devices, per_device(): lax.ppermute(other, 'chan', [(i, i ^ bit) for i in range(groups)])  8.09 us
    ppermute x3, starting transfers between devices, per_device(): lax.ppermute(other, 'chan', [(i, i ^ bit) for i in range(groups)])  7.69 us
    ppermute x1, waiting for transfers between devices, per_device(): received = lax.ppermute(send, 'chan', [(i, i ^ 1) for i in range(groups)])  1.28 us
    add x1, other arithmetic, per_device(): own = keep.astype(F32) + received.astype(F32)  0.97 us
    pallas_call x1, Pallas kernels, per_device(): pl.pallas_call(lambda *refs: finish_kernel(bins, 1.0 / math.sqrt(all_chan...  0.73 us
  transfers between devices with their start and end apart: 4, of which 4 were waited for; matrix products, arithmetic and copies ran while one was open for 0% of the time, Pallas kernels for 0%

profile of v2, /device:TPU:0, one launch (start us, length us, event | category | flops | bytes accessed | tf_op | source)
XLA Modules:
  0.0 34.2 jit_solution(5180676500302063519)
XLA Ops:
  0.6 14.2 %dedisperse.1 = (bf16[8,96,128]{2,1,0:T(8,128)(2,1)}, bf16[8,96,128]{2,1,0:T(8,128)(2,1)}) custom-call(s32[128,128]{1,0:T(8,128)} %bitcast.22, s32[1,256]{1,0:T(1,128)} %bitcast.23, bf16[96,2048]{1,0:T(8,128)(2,1)} %constant.65.clone.refs_2_, bf16[256,256]{1,0:T(8,128)(2,1)} %constant.66.clone.refs_3_, bf16[4,1024,2048]{2,1,0:T(8,128)(2,1)} %refs_4_.1), custom_call_target="tpu_custom_call" | custom-call | tf_op jit(solution)/shard_map/dedisperse/pallas_call | solution.py:314
  14.8 0.4 %collective-permute-start = (bf16[8,96,128]{2,1,0:T(8,128)(2,1)}, bf16[8,96,128]{2,1,0:T(8,128)(2,1)S(1)}, u32[]{:S(2)}, u32[]{:S(2)}) collective-permute-start(bf16[8,96,128]{2,1,0:T(8,128)(2,1)} %get-tuple-element.5), channel_id=1, source_target_pairs={{0,1},{1,0},{2,3},{3,2},{4,5},{5,4},{6,7},{7,6},{8,9},{9,8},{10,11... | collective-permute-start | bytes 589832 | tf_op jit(solution)/shard_map/ppermute | solution.py:351
  15.3 1.3 %collective-permute-done = bf16[8,96,128]{2,1,0:T(8,128)(2,1)S(1)} collective-permute-done((bf16[8,96,128]{2,1,0:T(8,128)(2,1)}, bf16[8,96,128]{2,1,0:T(8,128)(2,1)S(1)}, u32[]{:S(2)}, u32[]{:S(2)}) %collective-permute-start) | collective-permute-done | bytes 196640 | tf_op jit(solution)/shard_map/ppermute | solution.py:351
  16.6 1.0 %convert_add_fusion = f32[8,96,128]{2,1,0:T(8,128)S(1)} fusion(bf16[8,96,128]{2,1,0:T(8,128)(2,1)S(1)} %collective-permute-done, bf16[8,96,128]{2,1,0:T(8,128)(2,1)} %get-tuple-element.4), kind=kLoop, calls=%fused_computation | loop fusion | flops 294912 | bytes 786432 | tf_op jit(solution)/shard_map/add | solution.py:352
  17.6 3.0 %collective-permute-start.1 = (bf16[4,96,128]{2,1,0:T(8,128)(2,1)S(1)}, bf16[4,96,128]{2,1,0:T(8,128)(2,1)S(1)}, u32[]{:S(2)}, u32[]{:S(2)}) collective-permute-start(bf16[4,96,128]{2,1,0:T(8,128)(2,1)S(1)} %fusion), channel_id=1, source_target_pairs={{0,2},{1,3},{2,0},{3,1},{4,6},{5,7},{6,4},{7,5},{8,10},{9,11},{10,... | collective-permute-start | bytes 294920 | tf_op jit(solution)/shard_map/ppermute | solution.py:360
  20.5 3.1 %collective-permute-done.1 = bf16[4,96,128]{2,1,0:T(8,128)(2,1)S(1)} collective-permute-done((bf16[4,96,128]{2,1,0:T(8,128)(2,1)S(1)}, bf16[4,96,128]{2,1,0:T(8,128)(2,1)S(1)}, u32[]{:S(2)}, u32[]{:S(2)}) %collective-permute-start.1) | collective-permute-done | bytes 98336 | tf_op jit(solution)/shard_map/ppermute | solution.py:360
  23.7 1.9 %collective-permute-start.2 = (f32[2,96,128]{2,1,0:T(8,128)S(1)}, f32[2,96,128]{2,1,0:T(8,128)S(1)}, u32[]{:S(2)}, u32[]{:S(2)}) collective-permute-start(f32[2,96,128]{2,1,0:T(8,128)S(1)} %dynamic-slice_bitcast_fusion), channel_id=1, source_target_pairs={{0,4},{1,5},{2,6},{3,7},{4,0},{5,1},{6,2},{7,3},{8,12},{9,13},{10,... | collective-permute-start | bytes 294920 | tf_op jit(solution)/shard_map/ppermute | solution.py:360
  25.5 2.8 %collective-permute-done.2 = f32[2,96,128]{2,1,0:T(8,128)S(1)} collective-permute-done((f32[2,96,128]{2,1,0:T(8,128)S(1)}, f32[2,96,128]{2,1,0:T(8,128)S(1)}, u32[]{:S(2)}, u32[]{:S(2)}) %collective-permute-start.2) | collective-permute-done | bytes 98336 | tf_op jit(solution)/shard_map/ppermute | solution.py:360
  28.4 2.9 %collective-permute-start.3 = (f32[1,96,128]{2,1,0:T(8,128)S(1)}, f32[1,96,128]{2,1,0:T(8,128)S(1)}, u32[]{:S(2)}, u32[]{:S(2)}) collective-permute-start(f32[1,96,128]{2,1,0:T(8,128)S(1)} %constant_dynamic-slice_fusion), channel_id=1, source_target_pairs={{0,8},{1,9},{2,10},{3,11},{4,12},{5,13},{6,14},{7,15},{8,0},{9,1},... | collective-permute-start | bytes 147464 | tf_op jit(solution)/shard_map/ppermute | solution.py:360
  31.3 2.2 %collective-permute-done.3 = f32[1,96,128]{2,1,0:T(8,128)S(1)} collective-permute-done((f32[1,96,128]{2,1,0:T(8,128)S(1)}, f32[1,96,128]{2,1,0:T(8,128)S(1)}, u32[]{:S(2)}, u32[]{:S(2)}) %collective-permute-start.3) | collective-permute-done | bytes 49184 | tf_op jit(solution)/shard_map/ppermute | solution.py:360
  33.4 0.7 %finish.1 = (f32[3,2,4,256]{3,2,1,0:T(4,128)}, f32[4,16]{1,0:T(4,128)}) custom-call(f32[2,96,128]{2,1,0:T(8,128)S(1)} %bitcast_add_fusion.1.refs_0_, f32[96,128]{1,0:T(8,128)S(1)} %bitcast.17), custom_call_target="tpu_custom_call" | custom-call | tf_op jit(solution)/shard_map/finish/pallas_call | solution.py:365
  (5 shorter events, 0.1 us)
Async XLA Ops:
  14.8 1.7 %collective-permute-start = (bf16[8,96,128]{2,1,0:T(8,128)(2,1)}, bf16[8,96,128]{2,1,0:T(8,128)(2,1)S(1)}, u32[]{:S(2)}, u32[]{:S(2)}) collective-permute-start(bf16[8,96,128]{2,1,0:T(8,128)(2,1)} %get-tuple-element.5), channel_id=1, source_target_pairs={{0,1},{1,0},{2,3},{3,2},{4,5},{5,4},{6,7},{7,6},{8,9},{9,8},{10,11... | collective-permute-start | bytes 589832 | tf_op jit(solution)/shard_map/ppermute | solution.py:351
  17.6 6.1 %collective-permute-start.1 = (bf16[4,96,128]{2,1,0:T(8,128)(2,1)S(1)}, bf16[4,96,128]{2,1,0:T(8,128)(2,1)S(1)}, u32[]{:S(2)}, u32[]{:S(2)}) collective-permute-start(bf16[4,96,128]{2,1,0:T(8,128)(2,1)S(1)} %fusion), channel_id=1, source_target_pairs={{0,2},{1,3},{2,0},{3,1},{4,6},{5,7},{6,4},{7,5},{8,10},{9,11},{10,... | collective-permute-start | bytes 294920 | tf_op jit(solution)/shard_map/ppermute | solution.py:360
  23.7 4.7 %collective-permute-start.2 = (f32[2,96,128]{2,1,0:T(8,128)S(1)}, f32[2,96,128]{2,1,0:T(8,128)S(1)}, u32[]{:S(2)}, u32[]{:S(2)}) collective-permute-start(f32[2,96,128]{2,1,0:T(8,128)S(1)} %dynamic-slice_bitcast_fusion), channel_id=1, source_target_pairs={{0,4},{1,5},{2,6},{3,7},{4,0},{5,1},{6,2},{7,3},{8,12},{9,13},{10,... | collective-permute-start | bytes 294920 | tf_op jit(solution)/shard_map/ppermute | solution.py:360
  28.4 5.1 %collective-permute-start.3 = (f32[1,96,128]{2,1,0:T(8,128)S(1)}, f32[1,96,128]{2,1,0:T(8,128)S(1)}, u32[]{:S(2)}, u32[]{:S(2)}) collective-permute-start(f32[1,96,128]{2,1,0:T(8,128)S(1)} %constant_dynamic-slice_fusion), channel_id=1, source_target_pairs={{0,8},{1,9},{2,10},{3,11},{4,12},{5,13},{6,14},{7,15},{8,0},{9,1},... | collective-permute-start | bytes 147464 | tf_op jit(solution)/shard_map/ppermute | solution.py:360

commit v3 on v2

--- a/solution.py
+++ b/solution.py
@@ -87,7 +87,7 @@
     mix_ref,
 ):
     step = pl.program_id(0)
-    steps = pl.num_programs(0) - 1
+    steps = pl.num_programs(0)
     beams, block, samples = volt_ref.shape
     bins = acc_ref.shape[0]
     modulus = 2 * samples * SUBSTEPS
@@ -122,15 +122,21 @@
         return ladder(samples - 1)
 
     def spectrum(beam, middle):
-        part = lax.dot_general(
-            volt_ref[beam], table_ref[...], (((1,), (1,)), ((), ())), preferred_element_type=F32
-        ).T
-        part = (part * scale).astype(BF16).astype(F32)
-        zr, zi = turned(part[:bins], part[bins:], *middle)
-        for t in range(tiles):
-            lanes = slice(t * LANES, (t + 1) * LANES)
-            new_x_ref[t, beam] = zr[:, lanes]
-            new_x_ref[t, beams + beam] = zi[:, lanes]
+        many = 4
+        out = lax.dot_general(
+            volt_ref[beam : beam + many].reshape(many * block, samples),
+            table_ref[...],
+            (((1,), (1,)), ((), ())),
+            preferred_element_type=F32,
+        )
+        for n in range(many):
+            part = out[n * block : (n + 1) * block].T
+            part = (part * scale).astype(BF16).astype(F32)
+            zr, zi = turned(part[:bins], part[bins:], *middle)
+            for t in range(tiles):
+                lanes = slice(t * LANES, (t + 1) * LANES)
+                new_x_ref[t, beam + n] = zr[:, lanes]
+                new_x_ref[t, beams + beam + n] = zi[:, lanes]
 
     def spread(ref, r, f):
         return jnp.concatenate(
@@ -241,20 +247,20 @@
     def _():
         acc_ref[...] = jnp.zeros_like(acc_ref)
         middle = angles()
-        for beam in range(beams):
+        for beam in range(0, beams, 4):
             spectrum(beam, middle)
 
-    @pl.when((step > 0) & (step < steps))
+    @pl.when(step > 0)
     def _():
         unit = take()
         middle = angles()
         turn = start
         for quarter in range(4):
-            for beam in range(beams * quarter // 4, beams * (quarter + 1) // 4):
-                spectrum(beam, middle)
+            if quarter % 4 == 0:
+                spectrum(quarter, middle)
             turn = some_bins(quarter, turn, unit)
 
-    @pl.when(step == steps)
+    @pl.when(step == steps - 1)
     def _():
         unit = take()
         turn = start
@@ -270,13 +276,17 @@
     per = spin * 2 * beams
     half = lax.axis_size("chan") // 2
     mine = (lax.axis_index("chan") & half) // half
-    total = (own_ref[mine] + received_ref[...]) * chan_scale
+    first = per * (count // LANES)
+    received = received_ref[...].astype(F32)
+    received = jnp.concatenate(
+        [received[:first] + received[first : 2 * first], received[2 * first :]], axis=0
+    )
+    total = (own_ref[mine] + received) * chan_scale
     for h in range(count // LANES):
         for f in range(spin):
             for k in range(2):
                 row = h * per + (f * 2 + k) * beams
                 spectra_ref[f, k, :, h * LANES : (h + 1) * LANES] = total[row : row + beams]
-    first = per * (count // LANES)
     power = jnp.zeros((tper, LANES), F32)
     for m in range(rows // LANES):
         part = total[first + m * tper : first + (m + 1) * tper]
@@ -306,22 +316,21 @@
     rows = bins * rows8
     per = rows // groups
     tper = count // groups
-    out_rows = per * (count // LANES) + tper * (rows // LANES)
+    bins_rows = per * (count // LANES)
+    out_rows = bins_rows + tper * (rows // LANES)
 
     full = lambda *shape: pl.BlockSpec(shape, lambda i: (0,) * len(shape))
     vmem = pl.BlockSpec(memory_space=pltpu.VMEM)
     piece = jax.ShapeDtypeStruct((groups // 2, out_rows, LANES), BF16)
     keep, send = pl.pallas_call(
         lambda *refs: phase_kernel(groups, *refs),
-        grid=(steps + 1,),
+        grid=(steps,),
         in_specs=[
             full(all_chan // LANES, LANES),
             full(1, count),
             full(2 * bins, samples),
             full(256, 256),
-            pl.BlockSpec(
-                (beams, block, samples), lambda i: (0, jnp.minimum(i, steps - 1), 0)
-            ),
+            pl.BlockSpec((beams, block, samples), lambda i: (0, i, 0)),
         ],
         out_specs=[full(*piece.shape), full(*piece.shape)],
         out_shape=[piece, piece],
@@ -349,18 +358,31 @@
 
     index = lax.axis_index("chan")
     received = lax.ppermute(send, "chan", [(i, i ^ 1) for i in range(groups)])
-    own = keep.astype(F32) + received.astype(F32)
+    own = lax.optimization_barrier(keep.astype(F32)) + received.astype(F32)
     bit = 2
     while True:
         own = own.reshape(-1, 2, out_rows, LANES)
         mine = (index & bit) // bit
         other = lax.dynamic_index_in_dim(own, 1 - mine, 1, keepdims=False)
-        if bit == 2:
-            other = other.astype(BF16)
-        received = lax.ppermute(other, "chan", [(i, i ^ bit) for i in range(groups)])
+        if bit > 2:
+            whole = other[:, :bins_rows]
+            high = lax.reduce_precision(whole, exponent_bits=8, mantissa_bits=7)
+            other = jnp.concatenate([high, whole - high, other[:, bins_rows:]], axis=1)
+        received = lax.ppermute(
+            other.astype(BF16), "chan", [(i, i ^ bit) for i in range(groups)]
+        )
         if 2 * bit == groups:
             break
-        own = lax.dynamic_index_in_dim(own, mine, 1, keepdims=False) + received.astype(F32)
+        received = received.astype(F32)
+        if bit > 2:
+            received = jnp.concatenate(
+                [
+                    received[:, :bins_rows] + received[:, bins_rows : 2 * bins_rows],
+                    received[:, 2 * bins_rows :],
+                ],
+                axis=1,
+            )
+        own = lax.dynamic_index_in_dim(own, mine, 1, keepdims=False) + received
         bit *= 2
     return pl.pallas_call(
         lambda *refs: finish_kernel(bins, 1.0 / math.sqrt(all_chan), *refs),
@@ -372,7 +394,7 @@
         ],
         compiler_params=pltpu.CompilerParams(vmem_limit_bytes=4 << 20),
         name="finish",
-    )(own.reshape(2, out_rows, LANES), received.reshape(out_rows, LANES))
+    )(own.reshape(2, out_rows, LANES), received.reshape(out_rows + bins_rows, LANES))
 
 
 def solution(mesh):

time: 34.3 us -> 32.9 us (0.959)
  waiting for transfers between devices: 9.37 us -> 8 us
    ppermute x1, waiting for transfers between devices: 1.28 us -> 0.3 us  [per_device(): received = lax.ppermute(send, 'chan', [(i, i ^ 1) for i in range(groups)])]
    convert_element_type x0 -> x2, other arithmetic: none -> 0.96 us  [the longest x1 0.95 us: per_device(): own = lax.optimization_barrier(keep.astype(F32)) + received.astype(F32)]
    add x3 -> x4, other arithmetic: 1 us -> 0.08 us  [the longest x2 0.04 us: per_device(): own = lax.dynamic_index_in_dim(own, mine, 1, keepdims=False) + received]
    ppermute x3, waiting for transfers between devices: 8.09 us -> 7.7 us  [per_device(): lax.ppermute(other.astype(BF16), 'chan', [(i, i ^ bit) for i in range(gro...]
  transfers between devices with their start and end apart: 4 -> 4, of which waited for: 4 -> 4; matrix products, arithmetic and copies ran while one was open for 0% -> 3% of each run, Pallas kernels for 0% -> 0%
where the time goes in v3:
time: 32.9 us; the launch traced here: 32.7 us
  Pallas kernels  14.7 us (45%)
  starting transfers between devices  8.14 us (25%)
  waiting for transfers between devices  8 us (24%)
  other arithmetic  1.09 us (3%)
  between operations  0.75 us (2%)
    pallas_call x1, Pallas kernels, per_device(): pl.pallas_call(lambda *refs: phase_kernel(groups, *refs), grid=(steps,),...  13.9 us
    ppermute x3, waiting for transfers between devices, per_device(): lax.ppermute(other.astype(BF16), 'chan', [(i, i ^ bit) for i in range(gro...  7.7 us
    ppermute x3, starting transfers between devices, per_device(): lax.ppermute(other.astype(BF16), 'chan', [(i, i ^ bit) for i in range(gro...  7.69 us
    convert_element_type x1, other arithmetic, per_device(): own = lax.optimization_barrier(keep.astype(F32)) + received.astype(F32)  0.95 us
    pallas_call x1, Pallas kernels, per_device(): pl.pallas_call(lambda *refs: finish_kernel(bins, 1.0 / math.sqrt(all_chan...  0.73 us
  transfers between devices with their start and end apart: 4, of which 4 were waited for; matrix products, arithmetic and copies ran while one was open for 3% of the time, Pallas kernels for 0%

profile of v3, /device:TPU:0, one launch (start us, length us, event | category | flops | bytes accessed | tf_op | source)
XLA Modules:
  0.0 32.7 jit_solution(1807213540553549663)
XLA Ops:
  0.6 13.9 %dedisperse.1 = (bf16[8,96,128]{2,1,0:T(8,128)(2,1)}, bf16[8,96,128]{2,1,0:T(8,128)(2,1)}) custom-call(s32[128,128]{1,0:T(8,128)} %bitcast.22, s32[1,256]{1,0:T(1,128)} %bitcast.23, bf16[96,2048]{1,0:T(8,128)(2,1)} %constant.65.clone.refs_2_, bf16[256,256]{1,0:T(8,128)(2,1)} %constant.66.clone.refs_3_, bf16[4,1024,2048]{2,1,0:T(8,128)(2,1)} %refs_4_.1), custom_call_target="tpu_custom_call" | custom-call | tf_op jit(solution)/shard_map/dedisperse/pallas_call | solution.py:325
  14.6 0.5 %collective-permute-start = (bf16[8,96,128]{2,1,0:T(8,128)(2,1)}, bf16[8,96,128]{2,1,0:T(8,128)(2,1)S(1)}, u32[]{:S(2)}, u32[]{:S(2)}) collective-permute-start(bf16[8,96,128]{2,1,0:T(8,128)(2,1)} %get-tuple-element.5), channel_id=1, source_target_pairs={{0,1},{1,0},{2,3},{3,2},{4,5},{5,4},{6,7},{7,6},{8,9},{9,8},{10,11... | collective-permute-start | bytes 589832 | tf_op jit(solution)/shard_map/ppermute | solution.py:360
  15.0 1.0 %convert_element_type.28 = f32[8,96,128]{2,1,0:T(8,128)S(1)} convert(bf16[8,96,128]{2,1,0:T(8,128)(2,1)} %get-tuple-element.4) | non-fusion elementwise | flops 98304 | bytes 589824 | tf_op jit(solution)/shard_map/convert_element_type | solution.py:361
  16.0 0.3 collective-permute-done
  16.4 3.0 %collective-permute-start.1 = (bf16[4,96,128]{2,1,0:T(8,128)(2,1)S(1)}, bf16[4,96,128]{2,1,0:T(8,128)(2,1)S(1)}, u32[]{:S(2)}, u32[]{:S(2)}) collective-permute-start(bf16[4,96,128]{2,1,0:T(8,128)(2,1)S(1)} %fusion), channel_id=1, source_target_pairs={{0,2},{1,3},{2,0},{3,1},{4,6},{5,7},{6,4},{7,5},{8,10},{9,11},{10,... | collective-permute-start | bytes 294920 | tf_op jit(solution)/shard_map/ppermute | solution.py:371
  19.3 3.1 %collective-permute-done.1 = bf16[4,96,128]{2,1,0:T(8,128)(2,1)S(1)} collective-permute-done((bf16[4,96,128]{2,1,0:T(8,128)(2,1)S(1)}, bf16[4,96,128]{2,1,0:T(8,128)(2,1)S(1)}, u32[]{:S(2)}, u32[]{:S(2)}) %collective-permute-start.1) | collective-permute-done | bytes 98336 | tf_op jit(solution)/shard_map/ppermute | solution.py:371
  22.5 1.9 %collective-permute-start.2 = (bf16[2,144,128]{2,1,0:T(8,128)(2,1)S(1)}, bf16[2,144,128]{2,1,0:T(8,128)(2,1)S(1)}, u32[]{:S(2)}, u32[]{:S(2)}) collective-permute-start(bf16[2,144,128]{2,1,0:T(8,128)(2,1)S(1)} %pad_maximum_fusion), channel_id=1, source_target_pairs={{0,4},{1,5},{2,6},{3,7},{4,0},{5,1},{6,2},{7,3},{8,12},{9,13},{10,... | collective-permute-start | bytes 221192 | tf_op jit(solution)/shard_map/ppermute | solution.py:371
  24.4 2.6 %collective-permute-done.2 = bf16[2,144,128]{2,1,0:T(8,128)(2,1)S(1)} collective-permute-done((bf16[2,144,128]{2,1,0:T(8,128)(2,1)S(1)}, bf16[2,144,128]{2,1,0:T(8,128)(2,1)S(1)}, u32[]{:S(2)}, u32[]{:S(2)}) %collective-permute-start.2) | collective-permute-done | bytes 73760 | tf_op jit(solution)/shard_map/ppermute | solution.py:371
  27.1 2.9 %collective-permute-start.3 = (bf16[1,144,128]{2,1,0:T(8,128)(2,1)S(1)}, bf16[1,144,128]{2,1,0:T(8,128)(2,1)S(1)}, u32[]{:S(2)}, u32[]{:S(2)}) collective-permute-start(bf16[1,144,128]{2,1,0:T(8,128)(2,1)S(1)} %pad_maximum_fusion.1), channel_id=1, source_target_pairs={{0,8},{1,9},{2,10},{3,11},{4,12},{5,13},{6,14},{7,15},{8,0},{9,1},... | collective-permute-start | bytes 110600 | tf_op jit(solution)/shard_map/ppermute | solution.py:371
  29.9 2.0 %collective-permute-done.3 = bf16[1,144,128]{2,1,0:T(8,128)(2,1)S(1)} collective-permute-done((bf16[1,144,128]{2,1,0:T(8,128)(2,1)S(1)}, bf16[1,144,128]{2,1,0:T(8,128)(2,1)S(1)}, u32[]{:S(2)}, u32[]{:S(2)}) %collective-permute-start.3) | collective-permute-done | bytes 36896 | tf_op jit(solution)/shard_map/ppermute | solution.py:371
  32.0 0.7 %finish.1 = (f32[3,2,4,256]{3,2,1,0:T(4,128)}, f32[4,16]{1,0:T(4,128)}) custom-call(f32[2,96,128]{2,1,0:T(8,128)S(1)} %maximum_add_fusion.refs_0_, bf16[144,128]{1,0:T(8,128)(2,1)S(1)} %bitcast.17), custom_call_target="tpu_custom_call" | custom-call | tf_op jit(solution)/shard_map/finish/pallas_call | solution.py:387
  (14 shorter events, 0.2 us)
Async XLA Ops:
  14.6 1.7 %collective-permute-start = (bf16[8,96,128]{2,1,0:T(8,128)(2,1)}, bf16[8,96,128]{2,1,0:T(8,128)(2,1)S(1)}, u32[]{:S(2)}, u32[]{:S(2)}) collective-permute-start(bf16[8,96,128]{2,1,0:T(8,128)(2,1)} %get-tuple-element.5), channel_id=1, source_target_pairs={{0,1},{1,0},{2,3},{3,2},{4,5},{5,4},{6,7},{7,6},{8,9},{9,8},{10,11... | collective-permute-start | bytes 589832 | tf_op jit(solution)/shard_map/ppermute | solution.py:360
  16.4 6.1 %collective-permute-start.1 = (bf16[4,96,128]{2,1,0:T(8,128)(2,1)S(1)}, bf16[4,96,128]{2,1,0:T(8,128)(2,1)S(1)}, u32[]{:S(2)}, u32[]{:S(2)}) collective-permute-start(bf16[4,96,128]{2,1,0:T(8,128)(2,1)S(1)} %fusion), channel_id=1, source_target_pairs={{0,2},{1,3},{2,0},{3,1},{4,6},{5,7},{6,4},{7,5},{8,10},{9,11},{10,... | collective-permute-start | bytes 294920 | tf_op jit(solution)/shard_map/ppermute | solution.py:371
  22.5 4.4 %collective-permute-start.2 = (bf16[2,144,128]{2,1,0:T(8,128)(2,1)S(1)}, bf16[2,144,128]{2,1,0:T(8,128)(2,1)S(1)}, u32[]{:S(2)}, u32[]{:S(2)}) collective-permute-start(bf16[2,144,128]{2,1,0:T(8,128)(2,1)S(1)} %pad_maximum_fusion), channel_id=1, source_target_pairs={{0,4},{1,5},{2,6},{3,7},{4,0},{5,1},{6,2},{7,3},{8,12},{9,13},{10,... | collective-permute-start | bytes 221192 | tf_op jit(solution)/shard_map/ppermute | solution.py:371
  27.1 4.9 %collective-permute-start.3 = (bf16[1,144,128]{2,1,0:T(8,128)(2,1)S(1)}, bf16[1,144,128]{2,1,0:T(8,128)(2,1)S(1)}, u32[]{:S(2)}, u32[]{:S(2)}) collective-permute-start(bf16[1,144,128]{2,1,0:T(8,128)(2,1)S(1)} %pad_maximum_fusion.1), channel_id=1, source_target_pairs={{0,8},{1,9},{2,10},{3,11},{4,12},{5,13},{6,14},{7,15},{8,0},{9,1},... | collective-permute-start | bytes 110600 | tf_op jit(solution)/shard_map/ppermute | solution.py:371

commit v4 on v3

--- a/solution.py
+++ b/solution.py
@@ -359,29 +359,40 @@
     index = lax.axis_index("chan")
     received = lax.ppermute(send, "chan", [(i, i ^ 1) for i in range(groups)])
     own = lax.optimization_barrier(keep.astype(F32)) + received.astype(F32)
-    bit = 2
+    own = own.reshape(-1, 4, out_rows, LANES)
+    place = (index & 6) // 2
+    parts = [
+        lax.ppermute(
+            lax.dynamic_index_in_dim(own, place ^ k, 1, keepdims=False).astype(BF16),
+            "chan",
+            [(i, i ^ (2 * k)) for i in range(groups)],
+        )
+        for k in range(1, 4)
+    ]
+    own = lax.dynamic_index_in_dim(own, place, 1, keepdims=False)
+    for part in parts:
+        own = own + part.astype(F32)
+    bit = 8
     while True:
         own = own.reshape(-1, 2, out_rows, LANES)
         mine = (index & bit) // bit
         other = lax.dynamic_index_in_dim(own, 1 - mine, 1, keepdims=False)
-        if bit > 2:
-            whole = other[:, :bins_rows]
-            high = lax.reduce_precision(whole, exponent_bits=8, mantissa_bits=7)
-            other = jnp.concatenate([high, whole - high, other[:, bins_rows:]], axis=1)
+        whole = other[:, :bins_rows]
+        high = lax.reduce_precision(whole, exponent_bits=8, mantissa_bits=7)
+        other = jnp.concatenate([high, whole - high, other[:, bins_rows:]], axis=1)
         received = lax.ppermute(
             other.astype(BF16), "chan", [(i, i ^ bit) for i in range(groups)]
         )
         if 2 * bit == groups:
             break
         received = received.astype(F32)
-        if bit > 2:
-            received = jnp.concatenate(
-                [
-                    received[:, :bins_rows] + received[:, bins_rows : 2 * bins_rows],
-                    received[:, 2 * bins_rows :],
-                ],
-                axis=1,
-            )
+        received = jnp.concatenate(
+            [
+                received[:, :bins_rows] + received[:, bins_rows : 2 * bins_rows],
+                received[:, 2 * bins_rows :],
+            ],
+            axis=1,
+        )
         own = lax.dynamic_index_in_dim(own, mine, 1, keepdims=False) + received
         bit *= 2
     return pl.pallas_call(

time: 32.9 us -> 30.8 us (0.936)
  waiting for transfers between devices: 8 us -> 6.47 us
  starting transfers between devices: 8.14 us -> 7.72 us
    ppermute x3 -> x1, waiting for transfers between devices: 7.7 us -> 2.27 us  [per_device(): lax.ppermute(other.astype(BF16), 'chan', [(i, i ^ bit) for i in range(gro...]
    ppermute x3 -> x1, starting transfers between devices: 7.69 us -> 2.66 us  [per_device(): lax.ppermute(other.astype(BF16), 'chan', [(i, i ^ bit) for i in range(gro...]
    ppermute x0 -> x3, starting transfers between devices: none -> 4.61 us  [per_device(): lax.ppermute(lax.dynamic_index_in_dim(own, place ^ k, 1, keepdims=False)....]
    ppermute x0 -> x3, waiting for transfers between devices: none -> 3.89 us  [per_device(): lax.ppermute(lax.dynamic_index_in_dim(own, place ^ k, 1, keepdims=False)....]
  transfers between devices with their start and end apart: 4 -> 5, of which waited for: 4 -> 5; matrix products, arithmetic and copies ran while one was open for 3% -> 3% of each run, Pallas kernels for 0% -> 0%
where the time goes in v4:
time: 30.8 us; the launch traced here: 30.6 us
  Pallas kernels  14.6 us (47%)
  starting transfers between devices  7.72 us (25%)
  waiting for transfers between devices  6.47 us (21%)
  other arithmetic  1.03 us (3%)
  between operations  0.69 us (2%)
    pallas_call x1, Pallas kernels, per_device(): pl.pallas_call(lambda *refs: phase_kernel(groups, *refs), grid=(steps,),...  13.9 us
    ppermute x3, starting transfers between devices, per_device(): lax.ppermute(lax.dynamic_index_in_dim(own, place ^ k, 1, keepdims=False)....  4.61 us
    ppermute x3, waiting for transfers between devices, per_device(): lax.ppermute(lax.dynamic_index_in_dim(own, place ^ k, 1, keepdims=False)....  3.89 us
    ppermute x1, starting transfers between devices, per_device(): lax.ppermute(other.astype(BF16), 'chan', [(i, i ^ bit) for i in range(gro...  2.66 us
    ppermute x1, waiting for transfers between devices, per_device(): lax.ppermute(other.astype(BF16), 'chan', [(i, i ^ bit) for i in range(gro...  2.27 us
    convert_element_type x1, other arithmetic, per_device(): own = lax.optimization_barrier(keep.astype(F32)) + received.astype(F32)  0.95 us
    pallas_call x1, Pallas kernels, per_device(): pl.pallas_call(lambda *refs: finish_kernel(bins, 1.0 / math.sqrt(all_chan...  0.73 us
  transfers between devices with their start and end apart: 5, of which 5 were waited for; matrix products, arithmetic and copies ran while one was open for 3% of the time, Pallas kernels for 0%

profile of v4, /device:TPU:0, one launch (start us, length us, event | category | flops | bytes accessed | tf_op | source)
XLA Modules:
  0.0 30.6 jit_solution(4317867392460121060)
XLA Ops:
  0.6 13.9 %dedisperse.1 = (bf16[8,96,128]{2,1,0:T(8,128)(2,1)}, bf16[8,96,128]{2,1,0:T(8,128)(2,1)}) custom-call(s32[128,128]{1,0:T(8,128)} %bitcast.31, s32[1,256]{1,0:T(1,128)} %bitcast.32, bf16[96,2048]{1,0:T(8,128)(2,1)} %constant.55.clone.refs_2_, bf16[256,256]{1,0:T(8,128)(2,1)} %constant.56.clone.refs_3_, bf16[4,1024,2048]{2,1,0:T(8,128)(2,1)} %refs_4_.1), custom_call_target="tpu_custom_call" | custom-call | tf_op jit(solution)/shard_map/dedisperse/pallas_call | solution.py:325
  14.6 0.5 %collective-permute-start = (bf16[8,96,128]{2,1,0:T(8,128)(2,1)}, bf16[8,96,128]{2,1,0:T(8,128)(2,1)S(1)}, u32[]{:S(2)}, u32[]{:S(2)}) collective-permute-start(bf16[8,96,128]{2,1,0:T(8,128)(2,1)} %get-tuple-element.5), channel_id=1, source_target_pairs={{0,1},{1,0},{2,3},{3,2},{4,5},{5,4},{6,7},{7,6},{8,9},{9,8},{10,11... | collective-permute-start | bytes 589832 | tf_op jit(solution)/shard_map/ppermute | solution.py:360
  15.0 1.0 %convert_element_type.42 = f32[8,96,128]{2,1,0:T(8,128)S(1)} convert(bf16[8,96,128]{2,1,0:T(8,128)(2,1)} %get-tuple-element.4) | non-fusion elementwise | flops 98304 | bytes 589824 | tf_op jit(solution)/shard_map/convert_element_type | solution.py:361
  16.0 0.3 %collective-permute-done = bf16[8,96,128]{2,1,0:T(8,128)(2,1)S(1)} collective-permute-done((bf16[8,96,128]{2,1,0:T(8,128)(2,1)}, bf16[8,96,128]{2,1,0:T(8,128)(2,1)S(1)}, u32[]{:S(2)}, u32[]{:S(2)}) %collective-permute-start) | collective-permute-done | bytes 196640 | tf_op jit(solution)/shard_map/ppermute | solution.py:360
  16.4 4.0 %collective-permute-start.3 = (bf16[2,96,128]{2,1,0:T(8,128)(2,1)S(1)}, bf16[2,96,128]{2,1,0:T(8,128)(2,1)S(1)}, u32[]{:S(2)}, u32[]{:S(2)}) collective-permute-start(bf16[2,96,128]{2,1,0:T(8,128)(2,1)S(1)} %get-tuple-element.8), channel_id=1, source_target_pairs={{0,6},{1,7},{2,4},{3,5},{4,2},{5,3},{6,0},{7,1},{8,14},{9,15},{10,... | collective-permute-start | bytes 147464 | tf_op jit(solution)/shard_map/ppermute | solution.py:365
  20.3 0.4 %collective-permute-start.2 = (bf16[2,96,128]{2,1,0:T(8,128)(2,1)S(1)}, bf16[2,96,128]{2,1,0:T(8,128)(2,1)S(1)}, u32[]{:S(2)}, u32[]{:S(2)}) collective-permute-start(bf16[2,96,128]{2,1,0:T(8,128)(2,1)S(1)} %get-tuple-element.7), channel_id=1, source_target_pairs={{0,4},{1,5},{2,6},{3,7},{4,0},{5,1},{6,2},{7,3},{8,12},{9,13},{10,... | collective-permute-start | bytes 147464 | tf_op jit(solution)/shard_map/ppermute | solution.py:365
  20.8 0.2 collective-permute-start.1
  21.0 1.4 %collective-permute-done.3 = bf16[2,96,128]{2,1,0:T(8,128)(2,1)S(1)} collective-permute-done((bf16[2,96,128]{2,1,0:T(8,128)(2,1)S(1)}, bf16[2,96,128]{2,1,0:T(8,128)(2,1)S(1)}, u32[]{:S(2)}, u32[]{:S(2)}) %collective-permute-start.3) | collective-permute-done | bytes 49184 | tf_op jit(solution)/shard_map/ppermute | solution.py:365
  22.4 2.0 %collective-permute-done.2 = bf16[2,96,128]{2,1,0:T(8,128)(2,1)S(1)} collective-permute-done((bf16[2,96,128]{2,1,0:T(8,128)(2,1)S(1)}, bf16[2,96,128]{2,1,0:T(8,128)(2,1)S(1)}, u32[]{:S(2)}, u32[]{:S(2)}) %collective-permute-start.2) | collective-permute-done | bytes 49184 | tf_op jit(solution)/shard_map/ppermute | solution.py:365
  24.4 0.4 %collective-permute-done.1 = bf16[2,96,128]{2,1,0:T(8,128)(2,1)S(1)} collective-permute-done((bf16[2,96,128]{2,1,0:T(8,128)(2,1)S(1)}, bf16[2,96,128]{2,1,0:T(8,128)(2,1)S(1)}, u32[]{:S(2)}, u32[]{:S(2)}) %collective-permute-start.1) | collective-permute-done | bytes 49184 | tf_op jit(solution)/shard_map/ppermute | solution.py:365
  25.0 2.7 %collective-permute-start.4 = (bf16[1,144,128]{2,1,0:T(8,128)(2,1)S(1)}, bf16[1,144,128]{2,1,0:T(8,128)(2,1)S(1)}, u32[]{:S(2)}, u32[]{:S(2)}) collective-permute-start(bf16[1,144,128]{2,1,0:T(8,128)(2,1)S(1)} %pad_maximum_fusion), channel_id=1, source_target_pairs={{0,8},{1,9},{2,10},{3,11},{4,12},{5,13},{6,14},{7,15},{8,0},{9,1},... | collective-permute-start | bytes 110600 | tf_op jit(solution)/shard_map/ppermute | solution.py:383
  27.6 2.3 %collective-permute-done.4 = bf16[1,144,128]{2,1,0:T(8,128)(2,1)S(1)} collective-permute-done((bf16[1,144,128]{2,1,0:T(8,128)(2,1)S(1)}, bf16[1,144,128]{2,1,0:T(8,128)(2,1)S(1)}, u32[]{:S(2)}, u32[]{:S(2)}) %collective-permute-start.4) | collective-permute-done | bytes 36896 | tf_op jit(solution)/shard_map/ppermute | solution.py:383
  29.9 0.7 %finish.1 = (f32[3,2,4,256]{3,2,1,0:T(4,128)}, f32[4,16]{1,0:T(4,128)}) custom-call(f32[2,96,128]{2,1,0:T(8,128)S(1)} %fusion.1.refs_0_, bf16[144,128]{1,0:T(8,128)(2,1)S(1)} %bitcast.28), custom_call_target="tpu_custom_call" | custom-call | tf_op jit(solution)/shard_map/finish/pallas_call | solution.py:398
  (6 shorter events, 0.1 us)
Async XLA Ops:
  14.6 1.7 %collective-permute-start = (bf16[8,96,128]{2,1,0:T(8,128)(2,1)}, bf16[8,96,128]{2,1,0:T(8,128)(2,1)S(1)}, u32[]{:S(2)}, u32[]{:S(2)}) collective-permute-start(bf16[8,96,128]{2,1,0:T(8,128)(2,1)} %get-tuple-element.5), channel_id=1, source_target_pairs={{0,1},{1,0},{2,3},{3,2},{4,5},{5,4},{6,7},{7,6},{8,9},{9,8},{10,11... | collective-permute-start | bytes 589832 | tf_op jit(solution)/shard_map/ppermute | solution.py:360
  16.4 6.0 %collective-permute-start.3 = (bf16[2,96,128]{2,1,0:T(8,128)(2,1)S(1)}, bf16[2,96,128]{2,1,0:T(8,128)(2,1)S(1)}, u32[]{:S(2)}, u32[]{:S(2)}) collective-permute-start(bf16[2,96,128]{2,1,0:T(8,128)(2,1)S(1)} %get-tuple-element.8), channel_id=1, source_target_pairs={{0,6},{1,7},{2,4},{3,5},{4,2},{5,3},{6,0},{7,1},{8,14},{9,15},{10,... | collective-permute-start | bytes 147464 | tf_op jit(solution)/shard_map/ppermute | solution.py:365
  20.3 4.1 %collective-permute-start.2 = (bf16[2,96,128]{2,1,0:T(8,128)(2,1)S(1)}, bf16[2,96,128]{2,1,0:T(8,128)(2,1)S(1)}, u32[]{:S(2)}, u32[]{:S(2)}) collective-permute-start(bf16[2,96,128]{2,1,0:T(8,128)(2,1)S(1)} %get-tuple-element.7), channel_id=1, source_target_pairs={{0,4},{1,5},{2,6},{3,7},{4,0},{5,1},{6,2},{7,3},{8,12},{9,13},{10,... | collective-permute-start | bytes 147464 | tf_op jit(solution)/shard_map/ppermute | solution.py:365
  20.8 4.1 %collective-permute-start.1 = (bf16[2,96,128]{2,1,0:T(8,128)(2,1)S(1)}, bf16[2,96,128]{2,1,0:T(8,128)(2,1)S(1)}, u32[]{:S(2)}, u32[]{:S(2)}) collective-permute-start(bf16[2,96,128]{2,1,0:T(8,128)(2,1)S(1)} %get-tuple-element.6), channel_id=1, source_target_pairs={{0,2},{1,3},{2,0},{3,1},{4,6},{5,7},{6,4},{7,5},{8,10},{9,11},{10,... | collective-permute-start | bytes 147464 | tf_op jit(solution)/shard_map/ppermute | solution.py:365
  25.0 4.9 %collective-permute-start.4 = (bf16[1,144,128]{2,1,0:T(8,128)(2,1)S(1)}, bf16[1,144,128]{2,1,0:T(8,128)(2,1)S(1)}, u32[]{:S(2)}, u32[]{:S(2)}) collective-permute-start(bf16[1,144,128]{2,1,0:T(8,128)(2,1)S(1)} %pad_maximum_fusion), channel_id=1, source_target_pairs={{0,8},{1,9},{2,10},{3,11},{4,12},{5,13},{6,14},{7,15},{8,0},{9,1},... | collective-permute-start | bytes 110600 | tf_op jit(solution)/shard_map/ppermute | solution.py:383

commit v5 on v4

--- a/solution.py
+++ b/solution.py
@@ -269,12 +269,11 @@
         last()
 
 
-def finish_kernel(bins, chan_scale, own_ref, received_ref, spectra_ref, power_ref):
+def finish_kernel(bins, half, chan_scale, own_ref, received_ref, spectra_ref, power_ref):
     spin, _, beams, count = spectra_ref.shape
     tper = power_ref.shape[1]
     rows = bins * 2 * beams
     per = spin * 2 * beams
-    half = lax.axis_size("chan") // 2
     mine = (lax.axis_index("chan") & half) // half
     first = per * (count // LANES)
     received = received_ref[...].astype(F32)
@@ -359,21 +358,22 @@
     index = lax.axis_index("chan")
     received = lax.ppermute(send, "chan", [(i, i ^ 1) for i in range(groups)])
     own = lax.optimization_barrier(keep.astype(F32)) + received.astype(F32)
-    own = own.reshape(-1, 4, out_rows, LANES)
-    place = (index & 6) // 2
+    own = own.reshape(-1, 2, 2, 2, out_rows, LANES)
+    near, far = (index & 2) // 2, (index & 8) // 8
+
+    def share(k):
+        part = lax.dynamic_index_in_dim(own, far ^ (k // 8), 1, keepdims=False)
+        return lax.dynamic_index_in_dim(part, near ^ (k % 8 // 2), 2, keepdims=False)
+
     parts = [
-        lax.ppermute(
-            lax.dynamic_index_in_dim(own, place ^ k, 1, keepdims=False).astype(BF16),
-            "chan",
-            [(i, i ^ (2 * k)) for i in range(groups)],
-        )
-        for k in range(1, 4)
+        lax.ppermute(share(k).astype(BF16), "chan", [(i, i ^ k) for i in range(groups)])
+        for k in (2, 8, 10)
     ]
-    own = lax.dynamic_index_in_dim(own, place, 1, keepdims=False)
+    own = share(0)
     for part in parts:
         own = own + part.astype(F32)
-    bit = 8
-    while True:
+    bits = [4] + [16 << n for n in range(8) if 16 << n < groups]
+    for bit in bits:
         own = own.reshape(-1, 2, out_rows, LANES)
         mine = (index & bit) // bit
         other = lax.dynamic_index_in_dim(own, 1 - mine, 1, keepdims=False)
@@ -383,7 +383,7 @@
         received = lax.ppermute(
             other.astype(BF16), "chan", [(i, i ^ bit) for i in range(groups)]
         )
-        if 2 * bit == groups:
+        if bit == bits[-1]:
             break
         received = received.astype(F32)
         received = jnp.concatenate(
@@ -394,9 +394,8 @@
             axis=1,
         )
         own = lax.dynamic_index_in_dim(own, mine, 1, keepdims=False) + received
-        bit *= 2
     return pl.pallas_call(
-        lambda *refs: finish_kernel(bins, 1.0 / math.sqrt(all_chan), *refs),
+        lambda *refs: finish_kernel(bins, bits[-1], 1.0 / math.sqrt(all_chan), *refs),
         in_specs=[vmem, vmem],
         out_specs=[vmem, vmem],
         out_shape=[

time: 30.8 us -> 31.8 us (1.032)
  waiting for transfers between devices: 6.47 us -> 7.88 us
  starting transfers between devices: 7.72 us -> 7.29 us
    ppermute x1, starting transfers between devices: 2.66 us -> 1.21 us  [per_device(): lax.ppermute(other.astype(BF16), 'chan', [(i, i ^ bit) for i in range(gro...]
    ppermute x3, starting transfers between devices: 4.61 us -> 5.62 us  [per_device(): lax.ppermute(share(k).astype(BF16), 'chan', [(i, i ^ k) for i in range(gr...]
    ppermute x3, waiting for transfers between devices: 3.89 us -> 4.77 us  [per_device(): lax.ppermute(share(k).astype(BF16), 'chan', [(i, i ^ k) for i in range(gr...]
    ppermute x1, waiting for transfers between devices: 2.27 us -> 2.81 us  [per_device(): lax.ppermute(other.astype(BF16), 'chan', [(i, i ^ bit) for i in range(gro...]
  transfers between devices with their start and end apart: 5 -> 5, of which waited for: 5 -> 4; matrix products, arithmetic and copies ran while one was open for 3% -> 3% of each run, Pallas kernels for 0% -> 0%
where the time goes in v5:
time: 31.8 us; the launch traced here: 31.6 us
  Pallas kernels  14.6 us (46%)
  waiting for transfers between devices  7.88 us (25%)
  starting transfers between devices  7.29 us (23%)
  other arithmetic  1.03 us (3%)
  between operations  0.72 us (2%)
    pallas_call x1, Pallas kernels, per_device(): pl.pallas_call(lambda *refs: phase_kernel(groups, *refs), grid=(steps,),...  13.9 us
    ppermute x3, starting transfers between devices, per_device(): lax.ppermute(share(k).astype(BF16), 'chan', [(i, i ^ k) for i in range(gr...  5.62 us
    ppermute x3, waiting for transfers between devices, per_device(): lax.ppermute(share(k).astype(BF16), 'chan', [(i, i ^ k) for i in range(gr...  4.77 us
    ppermute x1, waiting for transfers between devices, per_device(): lax.ppermute(other.astype(BF16), 'chan', [(i, i ^ bit) for i in range(gro...  2.81 us
    ppermute x1, starting transfers between devices, per_device(): lax.ppermute(other.astype(BF16), 'chan', [(i, i ^ bit) for i in range(gro...  1.21 us
    convert_element_type x1, other arithmetic, per_device(): own = lax.optimization_barrier(keep.astype(F32)) + received.astype(F32)  0.95 us
    pallas_call x1, Pallas kernels, per_device(): pl.pallas_call(lambda *refs: finish_kernel(bins, bits[-1], 1.0 / math.sqr...  0.73 us
  transfers between devices with their start and end apart: 5, of which 4 were waited for; matrix products, arithmetic and copies ran while one was open for 3% of the time, Pallas kernels for 0%

profile of v5, /device:TPU:0, one launch (start us, length us, event | category | flops | bytes accessed | tf_op | source)
XLA Modules:
  0.0 31.6 jit_solution(16742141462272471570)
XLA Ops:
  0.6 13.9 %dedisperse.1 = (bf16[8,96,128]{2,1,0:T(8,128)(2,1)}, bf16[8,96,128]{2,1,0:T(8,128)(2,1)}) custom-call(s32[128,128]{1,0:T(8,128)} %bitcast.35, s32[1,256]{1,0:T(1,128)} %bitcast.36, bf16[96,2048]{1,0:T(8,128)(2,1)} %constant.183.clone.refs_2_, bf16[256,256]{1,0:T(8,128)(2,1)} %constant.184.clone.refs_3_, bf16[4,1024,2048]{2,1,0:T(8,128)(2,1)} %refs_4_.1), custom_call_target="tpu_custom_call" | custom-call | tf_op jit(solution)/shard_map/dedisperse/pallas_call | solution.py:324
  14.6 0.5 %collective-permute-start = (bf16[8,96,128]{2,1,0:T(8,128)(2,1)}, bf16[8,96,128]{2,1,0:T(8,128)(2,1)S(1)}, u32[]{:S(2)}, u32[]{:S(2)}) collective-permute-start(bf16[8,96,128]{2,1,0:T(8,128)(2,1)} %get-tuple-element.5), channel_id=1, source_target_pairs={{0,1},{1,0},{2,3},{3,2},{4,5},{5,4},{6,7},{7,6},{8,9},{9,8},{10,11... | collective-permute-start | bytes 589832 | tf_op jit(solution)/shard_map/ppermute | solution.py:359
  15.0 1.0 %convert_element_type.66 = f32[8,96,128]{2,1,0:T(8,128)S(1)} convert(bf16[8,96,128]{2,1,0:T(8,128)(2,1)} %get-tuple-element.4) | non-fusion elementwise | flops 98304 | bytes 589824 | tf_op jit(solution)/shard_map/convert_element_type | solution.py:360
  16.0 0.3 collective-permute-done
  16.4 5.0 %collective-permute-start.3 = (bf16[1,2,96,128]{3,2,1,0:T(8,128)(2,1)S(1)}, bf16[1,2,96,128]{3,2,1,0:T(8,128)(2,1)S(1)}, u32[]{:S(2)}, u32[]{:S(2)}) collective-permute-start(bf16[1,2,96,128]{3,2,1,0:T(8,128)(2,1)S(1)} %get-tuple-element.8), channel_id=1, source_target_pairs={{0,10},{1,11},{2,8},{3,9},{4,14},{5,15},{6,12},{7,13},{8,2},{9,3},... | collective-permute-start | bytes 147464 | tf_op jit(solution)/shard_map/ppermute | solution.py:369
  21.3 0.3 %collective-permute-start.2 = (bf16[1,2,96,128]{3,2,1,0:T(8,128)(2,1)S(1)}, bf16[1,2,96,128]{3,2,1,0:T(8,128)(2,1)S(1)}, u32[]{:S(2)}, u32[]{:S(2)}) collective-permute-start(bf16[1,2,96,128]{3,2,1,0:T(8,128)(2,1)S(1)} %get-tuple-element.7), channel_id=1, source_target_pairs={{0,8},{1,9},{2,10},{3,11},{4,12},{5,13},{6,14},{7,15},{8,0},{9,1},... | collective-permute-start | bytes 147464 | tf_op jit(solution)/shard_map/ppermute | solution.py:369
  21.7 0.3 collective-permute-start.1
  22.0 1.4 %collective-permute-done.3 = bf16[1,2,96,128]{3,2,1,0:T(8,128)(2,1)S(1)} collective-permute-done((bf16[1,2,96,128]{3,2,1,0:T(8,128)(2,1)S(1)}, bf16[1,2,96,128]{3,2,1,0:T(8,128)(2,1)S(1)}, u32[]{:S(2)}, u32[]{:S(2)}) %collective-permute-start.3) | collective-permute-done | bytes 49184 | tf_op jit(solution)/shard_map/ppermute | solution.py:369
  23.4 3.3 %collective-permute-done.2 = bf16[1,2,96,128]{3,2,1,0:T(8,128)(2,1)S(1)} collective-permute-done((bf16[1,2,96,128]{3,2,1,0:T(8,128)(2,1)S(1)}, bf16[1,2,96,128]{3,2,1,0:T(8,128)(2,1)S(1)}, u32[]{:S(2)}, u32[]{:S(2)}) %collective-permute-start.2) | collective-permute-done | bytes 49184 | tf_op jit(solution)/shard_map/ppermute | solution.py:369
  26.8 0.0 collective-permute-done.1
  26.9 1.2 %collective-permute-start.4 = (bf16[1,144,128]{2,1,0:T(8,128)(2,1)S(1)}, bf16[1,144,128]{2,1,0:T(8,128)(2,1)S(1)}, u32[]{:S(2)}, u32[]{:S(2)}) collective-permute-start(bf16[1,144,128]{2,1,0:T(8,128)(2,1)S(1)} %pad_maximum_fusion), channel_id=1, source_target_pairs={{0,4},{1,5},{2,6},{3,7},{4,0},{5,1},{6,2},{7,3},{8,12},{9,13},{10,... | collective-permute-start | bytes 110600 | tf_op jit(solution)/shard_map/ppermute | solution.py:383
  28.1 2.8 %collective-permute-done.4 = bf16[1,144,128]{2,1,0:T(8,128)(2,1)S(1)} collective-permute-done((bf16[1,144,128]{2,1,0:T(8,128)(2,1)S(1)}, bf16[1,144,128]{2,1,0:T(8,128)(2,1)S(1)}, u32[]{:S(2)}, u32[]{:S(2)}) %collective-permute-start.4) | collective-permute-done | bytes 36896 | tf_op jit(solution)/shard_map/ppermute | solution.py:383
  30.9 0.7 %finish.1 = (f32[3,2,4,256]{3,2,1,0:T(4,128)}, f32[4,16]{1,0:T(4,128)}) custom-call(f32[2,96,128]{2,1,0:T(8,128)S(1)} %bitcast.31, bf16[144,128]{1,0:T(8,128)(2,1)S(1)} %bitcast.32), custom_call_target="tpu_custom_call" | custom-call | tf_op jit(solution)/shard_map/finish/pallas_call | solution.py:397
  (7 shorter events, 0.1 us)
Async XLA Ops:
  14.6 1.7 %collective-permute-start = (bf16[8,96,128]{2,1,0:T(8,128)(2,1)}, bf16[8,96,128]{2,1,0:T(8,128)(2,1)S(1)}, u32[]{:S(2)}, u32[]{:S(2)}) collective-permute-start(bf16[8,96,128]{2,1,0:T(8,128)(2,1)} %get-tuple-element.5), channel_id=1, source_target_pairs={{0,1},{1,0},{2,3},{3,2},{4,5},{5,4},{6,7},{7,6},{8,9},{9,8},{10,11... | collective-permute-start | bytes 589832 | tf_op jit(solution)/shard_map/ppermute | solution.py:359
  16.4 7.1 %collective-permute-start.3 = (bf16[1,2,96,128]{3,2,1,0:T(8,128)(2,1)S(1)}, bf16[1,2,96,128]{3,2,1,0:T(8,128)(2,1)S(1)}, u32[]{:S(2)}, u32[]{:S(2)}) collective-permute-start(bf16[1,2,96,128]{3,2,1,0:T(8,128)(2,1)S(1)} %get-tuple-element.8), channel_id=1, source_target_pairs={{0,10},{1,11},{2,8},{3,9},{4,14},{5,15},{6,12},{7,13},{8,2},{9,3},... | collective-permute-start | bytes 147464 | tf_op jit(solution)/shard_map/ppermute | solution.py:369
  21.3 5.4 %collective-permute-start.2 = (bf16[1,2,96,128]{3,2,1,0:T(8,128)(2,1)S(1)}, bf16[1,2,96,128]{3,2,1,0:T(8,128)(2,1)S(1)}, u32[]{:S(2)}, u32[]{:S(2)}) collective-permute-start(bf16[1,2,96,128]{3,2,1,0:T(8,128)(2,1)S(1)} %get-tuple-element.7), channel_id=1, source_target_pairs={{0,8},{1,9},{2,10},{3,11},{4,12},{5,13},{6,14},{7,15},{8,0},{9,1},... | collective-permute-start | bytes 147464 | tf_op jit(solution)/shard_map/ppermute | solution.py:369
  21.7 5.1 %collective-permute-start.1 = (bf16[1,2,96,128]{3,2,1,0:T(8,128)(2,1)S(1)}, bf16[1,2,96,128]{3,2,1,0:T(8,128)(2,1)S(1)}, u32[]{:S(2)}, u32[]{:S(2)}) collective-permute-start(bf16[1,2,96,128]{3,2,1,0:T(8,128)(2,1)S(1)} %get-tuple-element.6), channel_id=1, source_target_pairs={{0,2},{1,3},{2,0},{3,1},{4,6},{5,7},{6,4},{7,5},{8,10},{9,11},{10,... | collective-permute-start | bytes 147464 | tf_op jit(solution)/shard_map/ppermute | solution.py:369
  26.9 4.0 %collective-permute-start.4 = (bf16[1,144,128]{2,1,0:T(8,128)(2,1)S(1)}, bf16[1,144,128]{2,1,0:T(8,128)(2,1)S(1)}, u32[]{:S(2)}, u32[]{:S(2)}) collective-permute-start(bf16[1,144,128]{2,1,0:T(8,128)(2,1)S(1)} %pad_maximum_fusion), channel_id=1, source_target_pairs={{0,4},{1,5},{2,6},{3,7},{4,0},{5,1},{6,2},{7,3},{8,12},{9,13},{10,... | collective-permute-start | bytes 110600 | tf_op jit(solution)/shard_map/ppermute | solution.py:383
